TPU v7x, 256 devices: a whole 4x4x8 slice. The times are simulated.
256 devices in a mesh: tm: 4 (over z_lo), space: 64 (over y, x, z_hi, core).
Axes of the slice: x: 4, y: 4, z: 8 (z_hi: 2, z_lo: 4; z = z_hi * 4 + z_lo), core: 2. Of those that a mesh axis runs over, the one named last changes fastest.
Arguments:
- initial: float32 [256, 256, 512], P('space'), may hold values from -6 to 6
- iterate: float32 [4, 256, 256, 512], P('tm', 'space'), may hold values from -6 to 6
- diffusivity: float32 [256, 256, 512], P('space'), may hold values from 0.25 to 1
Outputs:
- corrected: float32 [4, 256, 256, 512], P('tm', 'space')
All inputs are finite; a program needn't handle non-finite values.
Results may differ from a plain program's by a relative error of at most 0.0001.
Values sent between devices are 32-bit elements; how exact they have to be, the bound alone decides.
A program may use at most 128 MiB of HBM per device.

v0:
```python
import jax
import jax.numpy as jnp
from jax import lax
from jax.sharding import PartitionSpec as P

STEPS = 4


courant = 0.15


def extended(cells, sides, width):
    for axis, dim in sides:
        count = lax.axis_size(axis)
        ends = count - 1
        head = lax.slice_in_dim(cells, 0, width, axis=dim)
        tail = lax.slice_in_dim(cells, cells.shape[dim] - width, cells.shape[dim], axis=dim)
        cells = jnp.concatenate(
            [
                lax.ppermute(tail, axis, [(i, (i + 1) % count) for i in range(ends)]),
                cells,
                lax.ppermute(head, axis, [((i + 1) % count, i) for i in range(ends)]),
            ],
            axis=dim,
        )
    return cells


def shifted(x, axis, by):
    devices = lax.axis_size(axis)
    pairs = [(i, i + by) for i in range(devices) if 0 <= i + by < devices]
    return lax.ppermute(x, axis, pairs)


def advance(values, diffusivity):
    center = values[1:-1]
    coeff = diffusivity[1:-1]
    flux = (coeff + diffusivity[2:]) * (values[2:] - center) + (coeff + diffusivity[:-2]) * (
        values[:-2] - center
    )
    side_values = jnp.pad(center, ((0, 0), (1, 1), (0, 0)))
    side_coeff = jnp.pad(coeff, ((0, 0), (1, 1), (0, 0)))
    flux = (
        flux
        + (coeff + side_coeff[:, 2:]) * (side_values[:, 2:] - center)
        + (coeff + side_coeff[:, :-2]) * (side_values[:, :-2] - center)
    )
    cross_values = jnp.pad(center, ((0, 0), (0, 0), (1, 1)))
    cross_coeff = jnp.pad(coeff, ((0, 0), (0, 0), (1, 1)))
    flux = (
        flux
        + (coeff + cross_coeff[:, :, 2:]) * (cross_values[:, :, 2:] - center)
        + (coeff + cross_coeff[:, :, :-2]) * (cross_values[:, :, :-2] - center)
    )
    return center + 0.5 * courant * flux


def pair_matrix(width):
    fine_index = jnp.arange(width, dtype=jnp.int32)[:, None] // 2
    coarse_index = jnp.arange(width // 2, dtype=jnp.int32)[None, :]
    return (fine_index == coarse_index).astype(jnp.float32)


def restrict(values):
    depth_z, depth_y, depth_x = values.shape
    summed = values.reshape(depth_z // 2, 2, depth_y // 2, 2, depth_x).sum(axis=(1, 3))
    pairing = pair_matrix(depth_x)
    return 0.125 * jnp.dot(summed, pairing, precision=lax.Precision.HIGHEST)


def prolong(values):
    depth_z, depth_y, depth_x = values.shape
    pairing = pair_matrix(2 * depth_x)
    widened = jnp.dot(values, pairing.T, precision=lax.Precision.HIGHEST)
    spread = jnp.broadcast_to(widened[:, None, :, None, :], (depth_z, 2, depth_y, 2, 2 * depth_x))
    return spread.reshape(2 * depth_z, 2 * depth_y, 2 * depth_x)


def coarse_step(error, coarse_wide):
    padded = extended(error, (("space", 0),), 1)
    return advance(padded, coarse_wide)


def local(initial, iterate, diffusivity):
    planes = initial.shape[0]
    previous = shifted(iterate, "tm", 1)
    leading = lax.axis_index("tm") == 0
    begin_state = jnp.where(leading, initial, previous[0])
    margin = 2
    diff_wide = extended(diffusivity, (("space", 0),), margin)
    state = begin_state
    local_diff = diff_wide[margin - 1 : margin + planes + 1]
    for number in range(STEPS):
        padded = extended(state, (("space", 0),), 1)
        state = advance(padded, local_diff)
    residual = state - iterate[0]
    coarse_wide = restrict(diff_wide)
    restricted = restrict(residual)
    error = restricted
    power = restricted
    for offset in range(1, lax.axis_size("tm")):
        power = coarse_step(power, coarse_wide)
        error = error + shifted(power, "tm", offset)
    corrected = iterate[0] + prolong(error)
    return corrected[None]


def solution(mesh):
    placed = (P("space", None, None), P("tm", "space", None, None), P("space", None, None))
    return jax.shard_map(
        local, mesh=mesh, in_specs=placed, out_specs=P("tm", "space", None, None), check_vma=False
    )
```

profile of v0, /device:TPU:121, one launch (start us, length us, event | category | flops | bytes accessed | tf_op | source)
XLA Modules:
  0.0 315.0 jit_solution(793893072710296463)
XLA Ops:
  7.0 6.9 %collective-permute-start.3 = (f32[2,256,512]{2,1,0:T(8,128)}, f32[2,256,512]{2,1,0:T(8,128)}, u32[]{:S(2)}, u32[]{:S(2)}) collective-permute-start(f32[2,256,512]{2,1,0:T(8,128)} %get-tuple-element.16), channel_id=1, source_target_pairs={{0,1},{1,2},{2,3},{3,4},{4,5},{5,6},{6,7},{7,8},{8,9},{9,10},{10,1... | collective-permute-start | bytes 3145736 | tf_op jit(solution)/shard_map/ppermute | solution.py:20
  13.9 35.8 %collective-permute-done = f32[1,4,256,512]{3,2,1,0:T(8,128)} collective-permute-done((f32[1,4,256,512]{3,2,1,0:T(8,128)}, f32[1,4,256,512]{3,2,1,0:T(8,128)}, u32[]{:S(2)}, u32[]{:S(2)}) %collective-permute-start) | collective-permute-done | bytes 2097184 | tf_op jit(solution)/shard_map/ppermute | solution.py:32
  51.9 22.1 %collective-permute-start.2 = (f32[1,256,512]{2,1,0:T(8,128)S(1)}, f32[1,256,512]{2,1,0:T(8,128)S(1)}, u32[]{:S(2)}, u32[]{:S(2)}) collective-permute-start(f32[1,256,512]{2,1,0:T(8,128)S(1)} %get-tuple-element.18), channel_id=1, source_target_pairs={{1,0},{2,1},{3,2},{4,3},{5,4},{6,5},{7,6},{8,7},{9,8},{10,9},{11,1... | collective-permute-start | bytes 1572872 | tf_op jit(solution)/shard_map/ppermute | solution.py:22
  76.0 9.9 %collective-permute-done.4 = f32[1,256,512]{2,1,0:T(8,128)S(1)} collective-permute-done((f32[1,256,512]{2,1,0:T(8,128)S(1)}, f32[1,256,512]{2,1,0:T(8,128)S(1)}, u32[]{:S(2)}, u32[]{:S(2)}) %collective-permute-start.4) | collective-permute-done | bytes 524320 | tf_op jit(solution)/shard_map/ppermute | solution.py:20
  85.9 9.7 %fusion.7 = (f32[4,256,512]{2,1,0:T(8,128)}, f32[4,256,512]{2,1,0:T(8,128)S(1)}, f32[4,256,512]{2,1,0:T(8,128)S(1)}, f32[4,256,512]{2,1,0:T(8,128)S(1)}, f32[4,256,512]{2,1,0:T(8,128)}) fusion(f32[4,256,512]{2,1,0:T(8,128)} %copy-done.5, f32[1,256,512]{2,1,0:T(8,128)S(1)} %collective-permute-done.4, f32[1,256,512]{2,1,0:T(8,128)S(1)} %collective-permute-done.2, ...), kind=kLoop, calls=%fused_computation.18 | loop fusion | flops 15204352 | bytes 17825792 | tf_op jit(solution)/shard_map/add | solution.py:55
  97.9 7.7 %collective-permute-start.5 = (f32[1,256,512]{2,1,0:T(8,128)S(1)}, f32[1,256,512]{2,1,0:T(8,128)S(1)}, u32[]{:S(2)}, u32[]{:S(2)}) collective-permute-start(f32[1,256,512]{2,1,0:T(8,128)S(1)} %get-tuple-element.14), channel_id=1, source_target_pairs={{1,0},{2,1},{3,2},{4,3},{5,4},{6,5},{7,6},{8,7},{9,8},{10,9},{11,1... | collective-permute-start | bytes 1572872 | tf_op jit(solution)/shard_map/ppermute | solution.py:22
  108.4 4.9 %collective-permute-done.5 = f32[1,256,512]{2,1,0:T(8,128)S(1)} collective-permute-done((f32[1,256,512]{2,1,0:T(8,128)S(1)}, f32[1,256,512]{2,1,0:T(8,128)S(1)}, u32[]{:S(2)}, u32[]{:S(2)}) %collective-permute-start.5) | collective-permute-done | bytes 524320 | tf_op jit(solution)/shard_map/ppermute | solution.py:22
  113.3 6.2 %collective-permute-done.6 = f32[1,256,512]{2,1,0:T(8,128)S(1)} collective-permute-done((f32[1,256,512]{2,1,0:T(8,128)S(1)}, f32[1,256,512]{2,1,0:T(8,128)S(1)}, u32[]{:S(2)}, u32[]{:S(2)}) %collective-permute-start.6) | collective-permute-done | bytes 524320 | tf_op jit(solution)/shard_map/ppermute | solution.py:20
  119.5 8.1 %fusion.15 = f32[4,256,512]{2,1,0:T(8,128)S(1)} fusion(f32[4,256,512]{2,1,0:T(8,128)} %get-tuple-element.5, f32[4,256,512]{2,1,0:T(8,128)S(1)} %copy-done.4, f32[4,256,512]{2,1,0:T(8,128)S(1)} %get-tuple-element.8, f32[1,256,512]{2,1,0:T(8,128)S(1)} %collective-permute-done.6, f32[1,256,512]{2,1,0:T(8,128)S(1)} %collective-permute-done.5, ...), kind=kLoop, calls=%fused_computation.26 | loop fusion | flops 13107200 | bytes 17825792 | tf_op jit(solution)/shard_map/add | solution.py:55
  127.7 7.5 %collective-permute-start.7 = (f32[1,256,512]{2,1,0:T(8,128)S(1)}, f32[1,256,512]{2,1,0:T(8,128)S(1)}, u32[]{:S(2)}, u32[]{:S(2)}) collective-permute-start(f32[1,256,512]{2,1,0:T(8,128)S(1)} %get-tuple-element.12), channel_id=1, source_target_pairs={{1,0},{2,1},{3,2},{4,3},{5,4},{6,5},{7,6},{8,7},{9,8},{10,9},{11,1... | collective-permute-start | bytes 1572872 | tf_op jit(solution)/shard_map/ppermute | solution.py:22
  137.9 9.4 %collective-permute-done.7 = f32[1,256,512]{2,1,0:T(8,128)S(1)} collective-permute-done((f32[1,256,512]{2,1,0:T(8,128)S(1)}, f32[1,256,512]{2,1,0:T(8,128)S(1)}, u32[]{:S(2)}, u32[]{:S(2)}) %collective-permute-start.7) | collective-permute-done | bytes 524320 | tf_op jit(solution)/shard_map/ppermute | solution.py:22
  149.2 4.8 %fusion.23 = f32[4,256,512]{2,1,0:T(8,128)S(1)} fusion(f32[4,256,512]{2,1,0:T(8,128)S(1)} %fusion.15, f32[4,256,512]{2,1,0:T(8,128)S(1)} %copy-done.4, f32[4,256,512]{2,1,0:T(8,128)S(1)} %get-tuple-element.8, f32[1,256,512]{2,1,0:T(8,128)S(1)} %collective-permute-done.8, f32[1,256,512]{2,1,0:T(8,128)S(1)} %collective-permute-done.7, ...), kind=kLoop, calls=%fused_computation.34 | loop fusion | flops 13107200 | bytes 17825792 | tf_op jit(solution)/shard_map/add | solution.py:55
  156.4 8.3 %collective-permute-start.10 = (f32[1,256,512]{2,1,0:T(8,128)}, f32[1,256,512]{2,1,0:T(8,128)}, u32[]{:S(2)}, u32[]{:S(2)}) collective-permute-start(f32[1,256,512]{2,1,0:T(8,128)} %get-tuple-element.11), channel_id=1, source_target_pairs={{0,1},{1,2},{2,3},{3,4},{4,5},{5,6},{6,7},{7,8},{8,9},{9,10},{10,1... | collective-permute-start | bytes 1572872 | tf_op jit(solution)/shard_map/ppermute | solution.py:20
  164.7 13.5 %collective-permute-start.9 = (f32[1,256,512]{2,1,0:T(8,128)}, f32[1,256,512]{2,1,0:T(8,128)}, u32[]{:S(2)}, u32[]{:S(2)}) collective-permute-start(f32[1,256,512]{2,1,0:T(8,128)} %get-tuple-element.10), channel_id=1, source_target_pairs={{1,0},{2,1},{3,2},{4,3},{5,4},{6,5},{7,6},{8,7},{9,8},{10,9},{11,1... | collective-permute-start | bytes 1572872 | tf_op jit(solution)/shard_map/ppermute | solution.py:22
  178.2 4.0 %pad_maximum_fusion = f32[8,256,512]{2,1,0:T(8,128)} fusion(f32[2,256,512]{2,1,0:T(8,128)S(1)} %collective-permute-done.1, f32[4,256,512]{2,1,0:T(8,128)S(1)} %copy-done, f32[2,256,512]{2,1,0:T(8,128)} %collective-permute-done.3), kind=kLoop, calls=%fused_computation | loop fusion | flops 2097152 | bytes 8388608 | tf_op jit(solution)/shard_map/concatenate | solution.py:18
  182.2 5.8 %reshape.49 = f32[4,2,128,2,512]{4,3,2,1,0:T(2,128)} reshape(f32[8,256,512]{2,1,0:T(8,128)} %pad_maximum_fusion) | data formatting | bytes 8388608 | tf_op jit(solution)/shard_map/reshape | solution.py:66
  188.0 6.2 %reduce_sum.19 = f32[4,128,512]{2,1,0:T(8,128)} reduce(f32[4,2,128,2,512]{4,3,2,1,0:T(2,128)} %reshape.49, f32[]{:T(128)} %constant.31.clone.1), dimensions={1,3}, to_apply=%region_1.2 | reduce | flops 786432 | bytes 5242884 | tf_op jit(solution)/shard_map/reduce_sum | solution.py:66
  194.3 12.6 %fusion.32 = f32[4,256,512]{2,1,0:T(8,128)} fusion(f32[4,256,512]{2,1,0:T(8,128)} %copy-done.6, f32[4,256,512]{2,1,0:T(8,128)} %get-tuple-element.9, f32[4,256,512]{2,1,0:T(8,128)} %copy-done.3, f32[1,256,512]{2,1,0:T(8,128)} %collective-permute-done.10, f32[1,256,512]{2,1,0:T(8,128)} %collective-permute-done.9, f32[1,4,256,512]{3,2,1,0:T(8,128)} %param.4, ...), kind=kLoop, calls=%fused_computation.43 | loop fusion | flops 13631488 | bytes 19922944 | tf_op jit(solution)/shard_map/sub | solution.py:96
  213.5 10.6 %collective-permute-start.11 = (f32[1,128,256]{2,1,0:T(8,128)S(1)}, f32[1,128,256]{2,1,0:T(8,128)S(1)}, u32[]{:S(2)}, u32[]{:S(2)}) collective-permute-start(f32[1,128,256]{2,1,0:T(8,128)S(1)} %get-tuple-element.24), channel_id=1, source_target_pairs={{1,0},{2,1},{3,2},{4,3},{5,4},{6,5},{7,6},{8,7},{9,8},{10,9},{11,1... | collective-permute-start | bytes 393224 | tf_op jit(solution)/shard_map/ppermute | solution.py:22
  226.8 4.4 %collective-permute-done.12 = f32[1,128,256]{2,1,0:T(8,128)S(1)} collective-permute-done((f32[1,128,256]{2,1,0:T(8,128)S(1)}, f32[1,128,256]{2,1,0:T(8,128)S(1)}, u32[]{:S(2)}, u32[]{:S(2)}) %collective-permute-start.12) | collective-permute-done | bytes 131104 | tf_op jit(solution)/shard_map/ppermute | solution.py:20
  231.6 12.6 %collective-permute-start.14 = (f32[1,128,256]{2,1,0:T(8,128)S(1)}, f32[1,128,256]{2,1,0:T(8,128)S(1)}, u32[]{:S(2)}, u32[]{:S(2)}) collective-permute-start(f32[1,128,256]{2,1,0:T(8,128)S(1)} %get-tuple-element.22), channel_id=1, source_target_pairs={{1,0},{2,1},{3,2},{4,3},{5,4},{6,5},{7,6},{8,7},{9,8},{10,9},{11,1... | collective-permute-start | bytes 393224 | tf_op jit(solution)/shard_map/ppermute | solution.py:22
  249.1 10.6 %collective-permute-start.17 = (f32[1,128,256]{2,1,0:T(8,128)S(1)}, f32[1,128,256]{2,1,0:T(8,128)S(1)}, u32[]{:S(2)}, u32[]{:S(2)}) collective-permute-start(f32[1,128,256]{2,1,0:T(8,128)S(1)} %get-tuple-element.20), channel_id=1, source_target_pairs={{1,0},{2,1},{3,2},{4,3},{5,4},{6,5},{7,6},{8,7},{9,8},{10,9},{11,1... | collective-permute-start | bytes 393224 | tf_op jit(solution)/shard_map/ppermute | solution.py:22
  267.7 20.0 %collective-permute-done.13 = f32[2,128,256]{2,1,0:T(8,128)S(1)} collective-permute-done((f32[2,128,256]{2,1,0:T(8,128)S(1)}, f32[2,128,256]{2,1,0:T(8,128)S(1)}, u32[]{:S(2)}, u32[]{:S(2)}) %collective-permute-start.13) | collective-permute-done | bytes 262176 | tf_op jit(solution)/shard_map/ppermute | solution.py:32
  287.7 17.7 %collective-permute-done.16 = f32[2,128,256]{2,1,0:T(8,128)S(1)} collective-permute-done((f32[2,128,256]{2,1,0:T(8,128)S(1)}, f32[2,128,256]{2,1,0:T(8,128)S(1)}, u32[]{:S(2)}, u32[]{:S(2)}) %collective-permute-start.16) | collective-permute-done | bytes 262176 | tf_op jit(solution)/shard_map/ppermute | solution.py:32
  (65 shorter events, 55.2 us)
Async XLA Ops:
  0.0 49.7 %copy-start.9 = (f32[4,256,512]{2,1,0:T(8,128)S(1)}, f32[4,256,512]{2,1,0:T(8,128)}, u32[]{:S(2)}) copy-start(f32[4,256,512]{2,1,0:T(8,128)} %param.3) | copy-start | bytes 6291460
  0.0 49.7 %collective-permute-start = (f32[1,4,256,512]{3,2,1,0:T(8,128)}, f32[1,4,256,512]{3,2,1,0:T(8,128)}, u32[]{:S(2)}, u32[]{:S(2)}) collective-permute-start(f32[1,4,256,512]{3,2,1,0:T(8,128)} %param.4), channel_id=1, source_target_pairs={{0,64},{64,128},{128,192},{1,65},{65,129},{129,193},{2,66},{66,130... | collective-permute-start | bytes 6291464 | tf_op jit(solution)/shard_map/ppermute | solution.py:32
  4.5 71.5 %collective-permute-start.1 = (f32[2,256,512]{2,1,0:T(8,128)}, f32[2,256,512]{2,1,0:T(8,128)S(1)}, u32[]{:S(2)}, u32[]{:S(2)}) collective-permute-start(f32[2,256,512]{2,1,0:T(8,128)} %get-tuple-element.17), channel_id=1, source_target_pairs={{1,0},{2,1},{3,2},{4,3},{5,4},{6,5},{7,6},{8,7},{9,8},{10,9},{11,1... | collective-permute-start | bytes 3145736 | tf_op jit(solution)/shard_map/ppermute | solution.py:22
  7.0 68.9 %collective-permute-start.3 = (f32[2,256,512]{2,1,0:T(8,128)}, f32[2,256,512]{2,1,0:T(8,128)}, u32[]{:S(2)}, u32[]{:S(2)}) collective-permute-start(f32[2,256,512]{2,1,0:T(8,128)} %get-tuple-element.16), channel_id=1, source_target_pairs={{0,1},{1,2},{2,3},{3,4},{4,5},{5,6},{6,7},{7,8},{8,9},{9,10},{10,1... | collective-permute-start | bytes 3145736 | tf_op jit(solution)/shard_map/ppermute | solution.py:20
  51.9 24.0 %collective-permute-start.2 = (f32[1,256,512]{2,1,0:T(8,128)S(1)}, f32[1,256,512]{2,1,0:T(8,128)S(1)}, u32[]{:S(2)}, u32[]{:S(2)}) collective-permute-start(f32[1,256,512]{2,1,0:T(8,128)S(1)} %get-tuple-element.18), channel_id=1, source_target_pairs={{1,0},{2,1},{3,2},{4,3},{5,4},{6,5},{7,6},{8,7},{9,8},{10,9},{11,1... | collective-permute-start | bytes 1572872 | tf_op jit(solution)/shard_map/ppermute | solution.py:22
  74.0 11.9 %collective-permute-start.4 = (f32[1,256,512]{2,1,0:T(8,128)S(1)}, f32[1,256,512]{2,1,0:T(8,128)S(1)}, u32[]{:S(2)}, u32[]{:S(2)}) collective-permute-start(f32[1,256,512]{2,1,0:T(8,128)S(1)} %get-tuple-element.19), channel_id=1, source_target_pairs={{0,1},{1,2},{2,3},{3,4},{4,5},{5,6},{6,7},{7,8},{8,9},{9,10},{10,1... | collective-permute-start | bytes 1572872 | tf_op jit(solution)/shard_map/ppermute | solution.py:20
  95.6 53.6 %copy-start.1 = (f32[4,256,512]{2,1,0:T(8,128)}, f32[4,256,512]{2,1,0:T(8,128)S(1)}, u32[]{:S(2)}) copy-start(f32[4,256,512]{2,1,0:T(8,128)S(1)} %get-tuple-element.6) | copy-start | bytes 6291460
  95.6 53.5 %copy-start.2 = (f32[4,256,512]{2,1,0:T(8,128)}, f32[4,256,512]{2,1,0:T(8,128)S(1)}, u32[]{:S(2)}) copy-start(f32[4,256,512]{2,1,0:T(8,128)S(1)} %get-tuple-element.7) | copy-start | bytes 6291460
  95.6 53.5 %copy-start.3 = (f32[4,256,512]{2,1,0:T(8,128)}, f32[4,256,512]{2,1,0:T(8,128)S(1)}, u32[]{:S(2)}) copy-start(f32[4,256,512]{2,1,0:T(8,128)S(1)} %get-tuple-element.8) | copy-start | bytes 6291460
  97.9 15.4 %collective-permute-start.5 = (f32[1,256,512]{2,1,0:T(8,128)S(1)}, f32[1,256,512]{2,1,0:T(8,128)S(1)}, u32[]{:S(2)}, u32[]{:S(2)}) collective-permute-start(f32[1,256,512]{2,1,0:T(8,128)S(1)} %get-tuple-element.14), channel_id=1, source_target_pairs={{1,0},{2,1},{3,2},{4,3},{5,4},{6,5},{7,6},{8,7},{9,8},{10,9},{11,1... | collective-permute-start | bytes 1572872 | tf_op jit(solution)/shard_map/ppermute | solution.py:22
  105.6 13.9 %collective-permute-start.6 = (f32[1,256,512]{2,1,0:T(8,128)S(1)}, f32[1,256,512]{2,1,0:T(8,128)S(1)}, u32[]{:S(2)}, u32[]{:S(2)}) collective-permute-start(f32[1,256,512]{2,1,0:T(8,128)S(1)} %get-tuple-element.15), channel_id=1, source_target_pairs={{0,1},{1,2},{2,3},{3,4},{4,5},{5,6},{6,7},{7,8},{8,9},{9,10},{10,1... | collective-permute-start | bytes 1572872 | tf_op jit(solution)/shard_map/ppermute | solution.py:20
  127.7 19.6 %collective-permute-start.7 = (f32[1,256,512]{2,1,0:T(8,128)S(1)}, f32[1,256,512]{2,1,0:T(8,128)S(1)}, u32[]{:S(2)}, u32[]{:S(2)}) collective-permute-start(f32[1,256,512]{2,1,0:T(8,128)S(1)} %get-tuple-element.12), channel_id=1, source_target_pairs={{1,0},{2,1},{3,2},{4,3},{5,4},{6,5},{7,6},{8,7},{9,8},{10,9},{11,1... | collective-permute-start | bytes 1572872 | tf_op jit(solution)/shard_map/ppermute | solution.py:22
  135.2 14.0 %collective-permute-start.8 = (f32[1,256,512]{2,1,0:T(8,128)S(1)}, f32[1,256,512]{2,1,0:T(8,128)S(1)}, u32[]{:S(2)}, u32[]{:S(2)}) collective-permute-start(f32[1,256,512]{2,1,0:T(8,128)S(1)} %get-tuple-element.13), channel_id=1, source_target_pairs={{0,1},{1,2},{2,3},{3,4},{4,5},{5,6},{6,7},{7,8},{8,9},{9,10},{10,1... | collective-permute-start | bytes 1572872 | tf_op jit(solution)/shard_map/ppermute | solution.py:20
  156.4 37.9 %collective-permute-start.10 = (f32[1,256,512]{2,1,0:T(8,128)}, f32[1,256,512]{2,1,0:T(8,128)}, u32[]{:S(2)}, u32[]{:S(2)}) collective-permute-start(f32[1,256,512]{2,1,0:T(8,128)} %get-tuple-element.11), channel_id=1, source_target_pairs={{0,1},{1,2},{2,3},{3,4},{4,5},{5,6},{6,7},{7,8},{8,9},{9,10},{10,1... | collective-permute-start | bytes 1572872 | tf_op jit(solution)/shard_map/ppermute | solution.py:20
  164.7 29.6 %collective-permute-start.9 = (f32[1,256,512]{2,1,0:T(8,128)}, f32[1,256,512]{2,1,0:T(8,128)}, u32[]{:S(2)}, u32[]{:S(2)}) collective-permute-start(f32[1,256,512]{2,1,0:T(8,128)} %get-tuple-element.10), channel_id=1, source_target_pairs={{1,0},{2,1},{3,2},{4,3},{5,4},{6,5},{7,6},{8,7},{9,8},{10,9},{11,1... | collective-permute-start | bytes 1572872 | tf_op jit(solution)/shard_map/ppermute | solution.py:22
  213.5 13.3 %collective-permute-start.11 = (f32[1,128,256]{2,1,0:T(8,128)S(1)}, f32[1,128,256]{2,1,0:T(8,128)S(1)}, u32[]{:S(2)}, u32[]{:S(2)}) collective-permute-start(f32[1,128,256]{2,1,0:T(8,128)S(1)} %get-tuple-element.24), channel_id=1, source_target_pairs={{1,0},{2,1},{3,2},{4,3},{5,4},{6,5},{7,6},{8,7},{9,8},{10,9},{11,1... | collective-permute-start | bytes 393224 | tf_op jit(solution)/shard_map/ppermute | solution.py:22
  224.0 7.1 %collective-permute-start.12 = (f32[1,128,256]{2,1,0:T(8,128)S(1)}, f32[1,128,256]{2,1,0:T(8,128)S(1)}, u32[]{:S(2)}, u32[]{:S(2)}) collective-permute-start(f32[1,128,256]{2,1,0:T(8,128)S(1)} %get-tuple-element.25), channel_id=1, source_target_pairs={{0,1},{1,2},{2,3},{3,4},{4,5},{5,6},{6,7},{7,8},{8,9},{9,10},{10,1... | collective-permute-start | bytes 393224 | tf_op jit(solution)/shard_map/ppermute | solution.py:20
  231.6 14.5 %collective-permute-start.14 = (f32[1,128,256]{2,1,0:T(8,128)S(1)}, f32[1,128,256]{2,1,0:T(8,128)S(1)}, u32[]{:S(2)}, u32[]{:S(2)}) collective-permute-start(f32[1,128,256]{2,1,0:T(8,128)S(1)} %get-tuple-element.22), channel_id=1, source_target_pairs={{1,0},{2,1},{3,2},{4,3},{5,4},{6,5},{7,6},{8,7},{9,8},{10,9},{11,1... | collective-permute-start | bytes 393224 | tf_op jit(solution)/shard_map/ppermute | solution.py:22
  244.2 4.5 %collective-permute-start.15 = (f32[1,128,256]{2,1,0:T(8,128)S(1)}, f32[1,128,256]{2,1,0:T(8,128)S(1)}, u32[]{:S(2)}, u32[]{:S(2)}) collective-permute-start(f32[1,128,256]{2,1,0:T(8,128)S(1)} %get-tuple-element.23), channel_id=1, source_target_pairs={{0,1},{1,2},{2,3},{3,4},{4,5},{5,6},{6,7},{7,8},{8,9},{9,10},{10,1... | collective-permute-start | bytes 393224 | tf_op jit(solution)/shard_map/ppermute | solution.py:20
  249.1 15.4 %collective-permute-start.17 = (f32[1,128,256]{2,1,0:T(8,128)S(1)}, f32[1,128,256]{2,1,0:T(8,128)S(1)}, u32[]{:S(2)}, u32[]{:S(2)}) collective-permute-start(f32[1,128,256]{2,1,0:T(8,128)S(1)} %get-tuple-element.20), channel_id=1, source_target_pairs={{1,0},{2,1},{3,2},{4,3},{5,4},{6,5},{7,6},{8,7},{9,8},{10,9},{11,1... | collective-permute-start | bytes 393224 | tf_op jit(solution)/shard_map/ppermute | solution.py:22
  259.7 6.3 %collective-permute-start.18 = (f32[1,128,256]{2,1,0:T(8,128)S(1)}, f32[1,128,256]{2,1,0:T(8,128)S(1)}, u32[]{:S(2)}, u32[]{:S(2)}) collective-permute-start(f32[1,128,256]{2,1,0:T(8,128)S(1)} %get-tuple-element.21), channel_id=1, source_target_pairs={{0,1},{1,2},{2,3},{3,4},{4,5},{5,6},{6,7},{7,8},{8,9},{9,10},{10,1... | collective-permute-start | bytes 393224 | tf_op jit(solution)/shard_map/ppermute | solution.py:20
  261.6 26.1 %collective-permute-start.13 = (f32[2,128,256]{2,1,0:T(8,128)S(1)}, f32[2,128,256]{2,1,0:T(8,128)S(1)}, u32[]{:S(2)}, u32[]{:S(2)}) collective-permute-start(f32[2,128,256]{2,1,0:T(8,128)S(1)} %fusion.79), channel_id=1, source_target_pairs={{0,64},{64,128},{128,192},{1,65},{65,129},{129,193},{2,66},{66,130... | collective-permute-start | bytes 786440 | tf_op jit(solution)/shard_map/ppermute | solution.py:32
  262.9 42.5 %collective-permute-start.16 = (f32[2,128,256]{2,1,0:T(8,128)S(1)}, f32[2,128,256]{2,1,0:T(8,128)S(1)}, u32[]{:S(2)}, u32[]{:S(2)}) collective-permute-start(f32[2,128,256]{2,1,0:T(8,128)S(1)} %fusion.89), channel_id=1, source_target_pairs={{0,128},{64,192},{1,129},{65,193},{2,130},{66,194},{3,131},{67,195... | collective-permute-start | bytes 786440 | tf_op jit(solution)/shard_map/ppermute | solution.py:32
  266.4 39.1 %collective-permute-start.19 = (f32[2,128,256]{2,1,0:T(8,128)S(1)}, f32[2,128,256]{2,1,0:T(8,128)S(1)}, u32[]{:S(2)}, u32[]{:S(2)}) collective-permute-start(f32[2,128,256]{2,1,0:T(8,128)S(1)} %fusion.99), channel_id=1, source_target_pairs={{0,192},{1,193},{2,194},{3,195},{4,196},{5,197},{6,198},{7,199},{8... | collective-permute-start | bytes 786440 | tf_op jit(solution)/shard_map/ppermute | solution.py:32
  (6 other events, 103.8 us)
where the time goes:
time: 317 us; the launch traced here: 315 us
  starting transfers between devices  121 us (38%)
  waiting for transfers between devices  114 us (36%)
  other arithmetic  54.6 us (17%)
  local copies, waits for them, and re-layouts  21.8 us (7%)
    ppermute x8, starting transfers between devices, extended(): lax.ppermute(head, axis, [((i + 1) % count, i) for i in range(ends)])  87.1 us
    ppermute x4, waiting for transfers between devices, shifted(): return lax.ppermute(x, axis, pairs)  73.6 us
    ppermute x8, starting transfers between devices, extended(): lax.ppermute(tail, axis, [(i, (i + 1) % count) for i in range(ends)])  28.4 us
    ppermute x8, waiting for transfers between devices, extended(): lax.ppermute(tail, axis, [(i, (i + 1) % count) for i in range(ends)])  26.5 us
    add x6, other arithmetic, advance(): return center + 0.5 * courant * flux  23.8 us
    ppermute x8, waiting for transfers between devices, extended(): lax.ppermute(head, axis, [((i + 1) % count, i) for i in range(ends)])  14.3 us
    sub x1, other arithmetic, local(): residual = state - iterate[0]  12.6 us
    reduce_sum x2, other arithmetic, restrict(): values.reshape(depth_z // 2, 2, depth_y // 2, 2, depth_x).sum(axis=(1, 3))  8.77 us
  transfers between devices with their start and end apart: 20, of which 11 were waited for; matrix products, arithmetic and copies ran while one was open for 7% of the time, Pallas kernels for 0%

commit v1 on v0

v1 whole, which is shorter than its diff:
```python
import jax
import jax.numpy as jnp
from jax import lax
from jax.experimental import pallas as pl
from jax.experimental.pallas import tpu as pltpu
from jax.sharding import PartitionSpec as P

STEPS = 4
courant = 0.15
K = 0.5 * courant
F32 = jnp.float32
MESH = pl.DeviceIdType.MESH

Y, X = 256, 512
LT = X // 128
R = 32
RC = 16
CH = 12


def lanes(shape):
    return lax.broadcasted_iota(jnp.int32, shape, 1)


def subs(shape):
    return lax.broadcasted_iota(jnp.int32, shape, 0)


def at_right(v, by):
    n = v.shape[1]
    return jnp.where(lanes(v.shape) >= n - by, 0.0, pltpu.roll(v, n - by, axis=1))


def at_left(v, by):
    return jnp.where(lanes(v.shape) < by, 0.0, pltpu.roll(v, by, axis=1))


def from_below(v):
    return jnp.where(subs(v.shape) == 7, 0.0, pltpu.roll(v, 7, axis=0))


def from_above(v):
    return jnp.where(subs(v.shape) == 0, 0.0, pltpu.roll(v, 1, axis=0))


def even(shape):
    return (lanes(shape) & 1) == 0


def swap_pairs(v):
    n = v.shape[1]
    return jnp.where(even(v.shape), pltpu.roll(v, n - 1, axis=1), pltpu.roll(v, 1, axis=1))


def pack(a, b):
    n = a.shape[1]
    return jnp.where(even(a.shape), a + pltpu.roll(a, n - 1, axis=1), b + pltpu.roll(b, 1, axis=1))


def coarse_advance(c, c_up, c_dn, c_io, v, v_up, v_dn, v_io):
    flux = (c + at_right(c, 2)) * (at_right(v, 2) - v) + (c + at_left(c, 2)) * (at_left(v, 2) - v)
    flux = flux + (c + c_up) * (v_up - v) + (c + c_dn) * (v_dn - v)
    flux = flux + (c + swap_pairs(c)) * (swap_pairs(v) - v)
    flux = flux + (c + c_io) * (v_io - v)
    return v + K * flux


def main_kernel(
    ini,
    itr,
    dif,
    out,
    craw,
    uraw,
    cbuf,
    dg,
    kxp,
    kxm,
    ky,
    kz,
    w,
    inn,
    cc,
    ccp,
    icoarse,
    ipart,
    own,
    ext,
    ccb,
    cco,
    go,
    gx,
    eb,
    hlo,
    hhi,
    hp,
    hn,
    eout,
    ld_sem,
    icp,
    chs,
    chr_,
    ins,
    inr,
    pps,
    ppr,
    cbs,
    cbr,
    cor,
    gos,
    gor,
    gxs,
    gxr,
    hs,
    hr,
    eos,
    eor,
):
    t = lax.axis_index("tm")
    s = lax.axis_index("space")
    core = s % 2
    zhi = (s // 2) % 2
    col = s // 4
    z = zhi * 4 + t
    ncol = lax.axis_size("space") // 4
    partner = s + 1 - 2 * core
    cross_ok = jnp.logical_and(
        jnp.logical_or(core == 1, s > 0), jnp.logical_or(core == 0, s < 4 * ncol - 1)
    )
    cross = jnp.where(cross_ok, s - 1 + 2 * core, s)
    qcol = cross // 4
    qzhi = (cross // 2) % 2
    qcore = cross % 2

    def plane(p):
        return (3 - p) + core * (2 * p - 3)

    def dev(tt, ss):
        return {"tm": tt, "space": ss}

    barrier = pltpu.get_barrier_semaphore()

    @pl.loop(0, 16)
    def _(i):
        ti, si = i % 4, col * 4 + i // 4

        @pl.when(jnp.logical_not(jnp.logical_and(ti == t, si == s)))
        def _():
            pl.semaphore_signal(barrier, inc=1, device_id=dev(ti, si), device_id_type=MESH)

    lat_ok = jnp.logical_or(
        jnp.logical_and(core == 0, col > 0), jnp.logical_and(core == 1, col < ncol - 1)
    )
    lat_col = jnp.where(core == 0, col - 1, col + 1)

    @pl.when(lat_ok)
    def _():
        @pl.loop(0, 8)
        def _(i):
            si = lat_col * 4 + (i // 4) * 2 + 1 - core
            pl.semaphore_signal(barrier, inc=1, device_id=dev(i % 4, si), device_id_type=MESH)

    def own_c(p, q):
        return pltpu.make_async_copy(
            dif.at[plane(p), :, pl.ds(128 * q, 128)], craw.at[p, q], ld_sem.at[0]
        )

    def own_u(src, p, q):
        return pltpu.make_async_copy(
            src.at[plane(p), :, pl.ds(128 * q, 128)], uraw.at[p, q], ld_sem.at[1]
        )

    for p in range(4):
        for q in range(LT):
            own_c(p, q).start()

    @pl.when(t == 3)
    def _():
        for p in range(4):
            for q in range(LT):
                own_u(ini, p, q).start()

    @pl.when(t != 3)
    def _():
        for p in range(4):
            for q in range(LT):
                own_u(itr.at[0], p, q).start()

    pl.semaphore_wait(barrier, jnp.where(lat_ok, 23, 15))

    def inner_c(q):
        return pltpu.make_async_remote_copy(
            src_ref=dif.at[plane(0), :, pl.ds(128 * q, 128)],
            dst_ref=craw.at[7, q],
            send_sem=icp.at[0, q],
            recv_sem=icp.at[1, q],
            device_id=dev(t, partner),
            device_id_type=MESH,
        )

    for q in range(LT):
        inner_c(q).start()

    def first(ch, i):
        j, q = i // LT, i % LT
        return pltpu.make_async_remote_copy(
            src_ref=dif.at[plane(3 - j), pl.ds(128 * ch, 128), pl.ds(pl.multiple_of(128 * q, 128), 128)],
            dst_ref=craw.at[4 + j, q, pl.ds(128 * ch, 128), :],
            send_sem=chs.at[2 + ch, i],
            recv_sem=chr_.at[ch, i],
            device_id=dev(3 - 3 * ch, cross),
            device_id_type=MESH,
        )

    def relay(ch, i):
        j, q = i // LT, i % LT
        ref = craw.at[4 + j, q, pl.ds(128 * ch, 128), :]
        return pltpu.make_async_remote_copy(
            src_ref=ref,
            dst_ref=ref,
            send_sem=chs.at[ch, i],
            recv_sem=chr_.at[ch, i],
            device_id=dev(jnp.clip(t - 1 + 2 * ch, 0, 3), s),
            device_id_type=MESH,
        )

    starts = (t == 0, t == 3)
    sends_on = (t > 0, t < 3)

    @pl.when(cross_ok)
    def _():
        for ch in range(2):

            @pl.when(starts[ch])
            def _():
                @pl.loop(0, CH)
                def _(i):
                    first(ch, i).start()

    def to_rows(raw, p, dst, d):
        for q in range(LT):

            @pl.loop(0, R)
            def _(r):
                dst[d, r + 1, :, 128 * q : 128 * q + 128] = raw[p, q, pl.ds(r, 8, stride=R), :]

        edge_rows(dst, d)

    def edge_rows(dst, d):
        dst[d, 0] = from_above(dst[d, R])
        dst[d, R + 1] = from_below(dst[d, 1])

    held_c = craw.at[pl.ds(0, 4)]
    pltpu.make_async_copy(held_c, held_c, ld_sem.at[0]).wait()
    pltpu.make_async_copy(uraw, uraw, ld_sem.at[1]).wait()
    for p in range(4):
        to_rows(uraw, p, w.at[0], p)

    def inner_state(k):
        return pltpu.make_async_remote_copy(
            src_ref=w.at[k % 2, 0, pl.ds(1, R)],
            dst_ref=inn.at[k],
            send_sem=ins.at[k],
            recv_sem=inr.at[k],
            device_id=dev(t, partner),
            device_id_type=MESH,
        )

    inner_state(0).start()
    for p in range(4):
        to_rows(craw, p, cbuf, p)

    @pl.loop(0, RC)
    def _(r):
        def block(src, p):
            a = 2 * r + 1
            return (src[p, a] + src[p, a + 1]) + (src[p + 1, a] + src[p + 1, a + 1])

        cc[r] = 0.125 * pack(block(cbuf, 0), block(cbuf, 2))
        icoarse[r] = 0.125 * pack(block(w.at[0], 0), block(w.at[0], 2))

    def to_partner(i):
        src, dst = ((cc, ccp), (icoarse, ipart))[i]
        return pltpu.make_async_remote_copy(
            src_ref=src,
            dst_ref=dst,
            send_sem=pps.at[i],
            recv_sem=ppr.at[i],
            device_id=dev(t, partner),
            device_id_type=MESH,
        )

    to_partner(0).start()
    to_partner(1).start()

    off = (jnp.where(t == 0, 5, jnp.where(t == 1, 1, 0)), jnp.where(t == 3, 5, jnp.where(t == 2, 1, 0)))

    @pl.when(cross_ok)
    def _():
        @pl.loop(0, CH + 5)
        def _(n):
            for ch in range(2):
                i = n - off[ch]

                @pl.when(jnp.logical_and(i >= 0, i < CH))
                def _():
                    relay(ch, i).wait_recv()

                    @pl.when(sends_on[ch])
                    def _():
                        relay(ch, i).start()

    for q in range(LT):
        inner_c(q).wait_recv()
    to_rows(craw, 7, cbuf, 7)

    @pl.when(cross_ok)
    def _():
        for p in range(4, 7):
            to_rows(craw, p, cbuf, p)

    @pl.when(jnp.logical_not(cross_ok))
    def _():
        for p in range(4, 7):

            @pl.loop(0, R + 2)
            def _(r):
                cbuf[p, r] = jnp.zeros((8, X), F32)

    def cross_send(is_self, src, dst, ssem, rsem, to):
        @pl.when(is_self)
        def _():
            pltpu.make_async_copy(src, dst, rsem).start()

        @pl.when(jnp.logical_not(is_self))
        def _():
            pltpu.make_async_remote_copy(
                src_ref=src,
                dst_ref=dst,
                send_sem=ssem,
                recv_sem=rsem,
                device_id=to,
                device_id_type=MESH,
            ).start()

    def cross_sent(is_self, src, dst, ssem, rsem, to):
        @pl.when(jnp.logical_not(is_self))
        def _():
            pltpu.make_async_remote_copy(
                src_ref=src,
                dst_ref=dst,
                send_sem=ssem,
                recv_sem=rsem,
                device_id=to,
                device_id_type=MESH,
            ).wait_send()

    def cc_own(h, m):
        e = t + 4 * h
        sp = col * 4 + h * 2 + zhi
        row = (2 * e - 1 + m + RC) % RC
        return sp == s, cc.at[row], ccb.at[core, m], cbs.at[h, m], cbr.at[0], dev(t, sp)

    def cc_out(h):
        e = t + 4 * h
        sp = qcol * 4 + h * 2 + qzhi
        return sp == s, cc.at[pl.ds(2 * e, 2)], cco.at[qcore], cbs.at[h, 4], cor.at[qcore], dev(t, sp)

    for h in range(2):
        for m in range(4):
            cross_send(*cc_own(h, m))

        @pl.when(cross_ok)
        def _():
            cross_send(*cc_out(h))

    vflag = jnp.where(cross_ok, 1.0, 0.0).astype(F32)

    @pl.loop(0, R)
    def _(r):
        a = r + 1
        ln = lanes((8, X))
        czm = cbuf[7, a]
        c = cbuf[0, a]
        kzm = K * (czm + c)
        for p in range(7):
            right = K * (c + at_right(c, 1))
            left = K * (c + at_left(c, 1))
            up = K * (c + cbuf[p, a + 1])
            dn = K * (c + cbuf[p, a - 1])
            total = (right + left) + (up + dn) + kzm
            kxp[p, r] = jnp.where(ln == X - 1, 0.0, right)
            kxm[p, r] = jnp.where(ln == 0, 0.0, left)
            ky[p, r] = dn
            kz[p, r] = kzm * vflag if p == 4 else kzm
            if p < 6:
                cn = cbuf[p + 1, a]
                kzm = K * (c + cn)
                total = total + kzm
                c = cn
            dg[p, r] = 1.0 - total

    for p in range(7):
        ky[p, R] = K * (cbuf[p, R] + cbuf[p, R + 1])

    def cell(k, p, r, top):
        a = r + 1
        src = w.at[k % 2]
        v = src[p, a]
        new = dg[p, r] * v
        new = new + kxp[p, r] * pltpu.roll(v, X - 1, axis=1)
        new = new + kxm[p, r] * pltpu.roll(v, 1, axis=1)
        new = new + ky[p, r + 1] * src[p, a + 1]
        new = new + ky[p, r] * src[p, a - 1]
        below = inn[k, r] if p == 0 else src[p - 1, a]
        new = new + kz[p, r] * below
        if p < top:
            new = new + kz[p + 1, r] * src[p + 1, a]
        return new

    for k in range(STEPS - 1):
        top = 3 + k
        inner_state(k).wait_recv()
        dst = w.at[(k + 1) % 2]
        if k > 0:
            inner_state(k - 1).wait_send()

        @pl.loop(0, R)
        def _(r):
            dst[0, r + 1] = cell(k, 0, r, top)

        edge_rows(dst, 0)
        inner_state(k + 1).start()

        @pl.loop(0, R)
        def _(r):
            for p in range(1, top + 1):
                dst[p, r + 1] = cell(k, p, r, top)
            dst[top + 1, r + 1] = kz[top + 1, r] * w[k % 2, top, r + 1]

        for p in range(1, top + 2):
            edge_rows(dst, p)

    to_partner(0).wait_recv()
    to_partner(1).wait_recv()
    gflag = jnp.where(t == 3, 0.0, 1.0).astype(F32)
    inner_state(STEPS - 1).wait_recv()

    @pl.loop(0, RC)
    def _(rc):
        k = STEPS - 1
        acc = []
        for planes in ((0, 1), (2, 3), (4, 5), (6,)):
            tot = None
            for p in planes:
                for b in range(2):
                    v = cell(k, p, 2 * rc + b, 6)
                    tot = v if tot is None else tot + v
            acc.append(tot)
        ev = even((8, X))
        lo = jnp.maximum(rc - 1, 0)
        hi = jnp.minimum(rc + 1, RC - 1)

        def neighbours(ref):
            up, dn = ref[hi], ref[lo]
            up = jnp.where(rc == RC - 1, from_below(ref[0]), up)
            dn = jnp.where(rc == 0, from_above(ref[RC - 1]), dn)
            return up, dn

        a = 2 * rc + 1
        outer = (cbuf[4, a] + cbuf[4, a + 1]) + (cbuf[5, a] + cbuf[5, a + 1])
        c = cc[rc]
        c_up, c_dn = neighbours(cc)
        c_io = jnp.where(ev, ccp[rc], 0.125 * pack(outer, outer))
        v = icoarse[rc]
        v_up, v_dn = neighbours(icoarse)
        v_io = jnp.where(ev, ipart[rc], 0.0)
        back = coarse_advance(c, c_up, c_dn, c_io, v, v_up, v_dn, v_io)
        own[rc] = 0.125 * pack(acc[0], acc[1]) - gflag * back
        ext[rc] = 0.125 * pack(acc[3], acc[2]) - gflag * jnp.where(ev, 0.0, K * (c + c_io) * v)

    def o_send(e):
        sp = col * 4 + (e // 4) * 2 + zhi
        te = e % 4
        return (
            jnp.logical_and(sp == s, te == t),
            own.at[pl.ds(2 * e, 2)],
            go.at[t, core],
            gos.at[e],
            gor.at[0],
            dev(te, sp),
        )

    def x_send(e):
        sp = qcol * 4 + (e // 4) * 2 + qzhi
        te = e % 4
        return (
            jnp.logical_and(sp == s, te == t),
            ext.at[pl.ds(2 * e, 2)],
            gx.at[qcore, t],
            gxs.at[e],
            gxr.at[qcore],
            dev(te, sp),
        )

    @pl.loop(0, 8)
    def _(i):
        e = (z + 4 + i) % 8
        cross_send(*o_send(e))

        @pl.when(cross_ok)
        def _():
            cross_send(*x_send(e))

    prev_ok = jnp.logical_or(core == 1, col > 0)
    next_ok = jnp.logical_or(core == 0, col < ncol - 1)
    prev_sp = jnp.where(core == 1, s - 1, jnp.maximum(col - 1, 0) * 4 + zhi * 2 + 1)
    next_sp = jnp.where(core == 0, s + 1, jnp.minimum(col + 1, ncol - 1) * 4 + zhi * 2)
    side_ok = (prev_ok, next_ok)

    pltpu.make_async_copy(ccb, ccb, cbr.at[0]).wait()
    for j in range(2):

        @pl.when(side_ok[j])
        def _():
            pltpu.make_async_copy(cco.at[j], cco.at[j], cor.at[j]).wait()

        @pl.when(jnp.logical_not(side_ok[j]))
        def _():
            cco[j] = jnp.zeros((2, 8, X), F32)
            gx[j] = jnp.zeros((4, 2, 8, X), F32)

    pltpu.make_async_copy(go, go, gor.at[0]).wait()
    for j in range(2):

        @pl.when(side_ok[j])
        def _():
            pltpu.make_async_copy(gx.at[j], gx.at[j], gxr.at[j]).wait()

    zu, zd = (z + 1) % 8, (z + 7) % 8

    def e_halo(k, kind):
        if kind == 0:
            src, dst, to = eb.at[k, 0], hhi.at[k], dev(zd % 4, col * 4 + (zd // 4) * 2 + core)
        elif kind == 1:
            src, dst, to = eb.at[k, 1], hlo.at[k], dev(zu % 4, col * 4 + (zu // 4) * 2 + core)
        elif kind == 2:
            src, dst, to = eb.at[k, :, 0], hn.at[k], dev(t, prev_sp)
        else:
            src, dst, to = eb.at[k, :, 1], hp.at[k], dev(t, next_sp)
        return pltpu.make_async_remote_copy(
            src_ref=src,
            dst_ref=dst,
            send_sem=hs.at[k, kind],
            recv_sem=hr.at[k, kind],
            device_id=to,
            device_id_type=MESH,
        )

    def e_back(k, j):
        sp = col * 4 + core * 2 + j
        return (
            jnp.logical_and(sp == s, t == k),
            eb.at[k, :, j],
            eout.at[pl.ds(2 * z, 2)],
            eos.at[k, j],
            eor.at[0],
            dev(k, sp),
        )

    for b in range(2):
        for j in range(2):
            eb[0, b, j] = go[3, j, b] + gx[j, 3, b]

    def send_level(k):
        if k < 3:
            e_halo(k, 0).start()
            e_halo(k, 1).start()

            @pl.when(prev_ok)
            def _():
                e_halo(k, 2).start()

            @pl.when(next_ok)
            def _():
                e_halo(k, 3).start()

        for j in range(2):
            cross_send(*e_back(k, j))

    send_level(0)
    for k in range(3):
        e_halo(k, 0).wait_recv()
        e_halo(k, 1).wait_recv()

        @pl.when(next_ok)
        def _():
            e_halo(k, 2).wait_recv()

        @pl.when(prev_ok)
        def _():
            e_halo(k, 3).wait_recv()

        @pl.when(jnp.logical_not(next_ok))
        def _():
            hn[k] = jnp.zeros((2, 8, X), F32)

        @pl.when(jnp.logical_not(prev_ok))
        def _():
            hp[k] = jnp.zeros((2, 8, X), F32)

        ev = even((8, X))
        for j in range(2):
            lo = hlo[k, j]
            hi = hhi[k, j]
            lo = jnp.where(z == 0, from_above(lo), lo)
            hi = jnp.where(z == 7, from_below(hi), hi)
            c_lo = jnp.where(z == 0, from_above(ccb[j, 0]), ccb[j, 0])
            c_hi = jnp.where(z == 7, from_below(ccb[j, 3]), ccb[j, 3])
            vs = (lo, eb[k, 0, j], eb[k, 1, j], hi)
            cs = (c_lo, ccb[j, 1], ccb[j, 2], c_hi)
            for b in range(2):
                far = hp[k, b] if j == 0 else hn[k, b]
                v_io = jnp.where(ev, eb[k, b, 1 - j], far)
                c_io = jnp.where(ev, ccb[1 - j, b + 1], cco[j, b])
                new = coarse_advance(
                    cs[b + 1], cs[b + 2], cs[b], c_io, vs[b + 1], vs[b + 2], vs[b], v_io
                )
                eb[k + 1, b, j] = new + (go[k, j, b] + gx[j, k, b])
        send_level(k + 1)

    pltpu.make_async_copy(eout, eout, eor.at[0]).wait()
    out[...] = eout[...]

    for q in range(LT):
        inner_c(q).wait_send()
    for k in range(STEPS - 2, STEPS):
        inner_state(k).wait_send()
    for i in range(2):
        to_partner(i).wait_send()

    @pl.when(cross_ok)
    def _():
        for ch in range(2):

            @pl.when(starts[ch])
            def _():
                @pl.loop(0, CH)
                def _(i):
                    first(ch, i).wait_send()

            @pl.when(sends_on[ch])
            def _():
                @pl.loop(0, CH)
                def _(i):
                    relay(ch, i).wait_send()

    for h in range(2):
        for m in range(4):
            cross_sent(*cc_own(h, m))

        @pl.when(cross_ok)
        def _():
            cross_sent(*cc_out(h))

    @pl.loop(0, 8)
    def _(e):
        cross_sent(*o_send(e))

        @pl.when(cross_ok)
        def _():
            cross_sent(*x_send(e))

    for k in range(3):
        e_halo(k, 0).wait_send()
        e_halo(k, 1).wait_send()

        @pl.when(prev_ok)
        def _():
            e_halo(k, 2).wait_send()

        @pl.when(next_ok)
        def _():
            e_halo(k, 3).wait_send()

    for k in range(4):
        for j in range(2):
            cross_sent(*e_back(k, j))


def final_kernel(itr, e, out, raw, res, isem, osem):
    core = lax.axis_index("space") % 2

    def plane(p):
        return (3 - p) + core * (2 * p - 3)

    def load(q):
        return pltpu.make_async_copy(itr.at[0, :, :, pl.ds(128 * q, 128)], raw.at[q], isem.at[q])

    def store(q):
        return pltpu.make_async_copy(res.at[q], out.at[0, :, :, pl.ds(128 * q, 128)], osem.at[q])

    for q in range(LT):
        load(q).start()
    for q in range(LT):
        load(q).wait()

        @pl.loop(0, RC)
        def _(r):
            rows = [[raw[q, plane(p), pl.ds(2 * r + b, 8, stride=R), :] for b in range(2)] for p in range(4)]
            a = (rows[0][0] + rows[0][1]) + (rows[1][0] + rows[1][1])
            c = (rows[2][0] + rows[2][1]) + (rows[3][0] + rows[3][1])
            d = e[r, :, 128 * q : 128 * q + 128] - 0.125 * pack(a, c)
            ev = even(d.shape)
            halves = (
                jnp.where(ev, d, pltpu.roll(d, 1, axis=1)),
                jnp.where(ev, pltpu.roll(d, 127, axis=1), d),
            )
            for p in range(4):
                for b in range(2):
                    res[q, plane(p), pl.ds(2 * r + b, 8, stride=R), :] = rows[p][b] + halves[p // 2]

        store(q).start()
    for q in range(LT):
        store(q).wait()


def local(initial, iterate, diffusivity):
    vm = lambda *shape: pltpu.VMEM(shape, F32)
    dma = lambda *shape: pltpu.SemaphoreType.DMA(shape)
    hbm = pl.BlockSpec(memory_space=pl.ANY)
    vmem = pl.BlockSpec(memory_space=pltpu.VMEM)
    err = pl.pallas_call(
        main_kernel,
        out_shape=jax.ShapeDtypeStruct((RC, 8, X), F32),
        in_specs=[hbm] * 3,
        out_specs=vmem,
        scratch_shapes=[
            vm(8, LT, Y, 128),
            vm(4, LT, Y, 128),
            vm(8, R + 2, 8, X),
            vm(7, R, 8, X),
            vm(7, R, 8, X),
            vm(7, R, 8, X),
            vm(7, R + 1, 8, X),
            vm(7, R, 8, X),
            vm(2, 7, R + 2, 8, X),
            vm(STEPS, R, 8, X),
            vm(RC, 8, X),
            vm(RC, 8, X),
            vm(RC, 8, X),
            vm(RC, 8, X),
            vm(RC, 8, X),
            vm(RC, 8, X),
            vm(2, 4, 8, X),
            vm(2, 2, 8, X),
            vm(4, 2, 2, 8, X),
            vm(2, 4, 2, 8, X),
            vm(4, 2, 2, 8, X),
            vm(3, 2, 8, X),
            vm(3, 2, 8, X),
            vm(3, 2, 8, X),
            vm(3, 2, 8, X),
            vm(RC, 8, X),
            dma(2),
            dma(2, LT),
            dma(4, CH),
            dma(2, CH),
            dma(STEPS),
            dma(STEPS),
            dma(2),
            dma(2),
            dma(2, 5),
            dma(1),
            dma(2),
            dma(8),
            dma(1),
            dma(8),
            dma(2),
            dma(3, 4),
            dma(3, 4),
            dma(4, 2),
            dma(1),
        ],
        compiler_params=pltpu.CompilerParams(
            collective_id=0, has_side_effects=True, vmem_limit_bytes=60 * 2**20
        ),
    )(initial, iterate, diffusivity)
    return pl.pallas_call(
        final_kernel,
        out_shape=jax.ShapeDtypeStruct(iterate.shape, F32),
        in_specs=[hbm, vmem],
        out_specs=hbm,
        scratch_shapes=[vm(LT, 4, Y, 128), vm(LT, 4, Y, 128), dma(LT), dma(LT)],
        compiler_params=pltpu.CompilerParams(vmem_limit_bytes=16 * 2**20),
    )(iterate, err)


def solution(mesh):
    placed = (P("space", None, None), P("tm", "space", None, None), P("space", None, None))
    return jax.shard_map(
        local, mesh=mesh, in_specs=placed, out_specs=P("tm", "space", None, None), check_vma=False
    )
```

time: 317 us -> 133 us (0.42)
  Pallas kernels: 0 us -> 132 us
  starting transfers between devices: 121 us -> 0 us
  waiting for transfers between devices: 114 us -> 0 us
  other arithmetic: 54.6 us -> 0 us
  local copies, waits for them, and re-layouts: 21.8 us -> 0.95 us
    pallas_call x0 -> x2, Pallas kernels: none -> 132 us  [the longest x1 119 us: local(): pl.pallas_call(main_kernel, out_shape=jax.ShapeDtypeStruct((RC, 8, X), F3...]
    ppermute x20 -> x0, starting transfers between devices: 121 us -> none  [the longest x8 87.1 us: extended(): lax.ppermute(head, axis, [((i + 1) % count, i) for i in range(ends)])]
    ppermute x20 -> x0, waiting for transfers between devices: 114 us -> none  [the longest x4 73.6 us: shifted(): return lax.ppermute(x, axis, pairs)]
    add x7 -> x0, other arithmetic: 27.2 us -> none  [the longest x6 23.8 us: advance(): return center + 0.5 * courant * flux]
    sub x1 -> x0, other arithmetic: 12.6 us -> none  [local(): residual = state - iterate[0]]
    reshape x3 -> x0, local copies, waits for them, and re-layouts: 12.1 us -> none  [the longest x2 8.3 us: restrict(): values.reshape(depth_z // 2, 2, depth_y // 2, 2, depth_x).sum(axis=(1, 3))]
    reduce_sum x2 -> x0, other arithmetic: 8.77 us -> none  [restrict(): values.reshape(depth_z // 2, 2, depth_y // 2, 2, depth_x).sum(axis=(1, 3))]
    slice x9 -> x0, local copies, waits for them, and re-layouts: 6.54 us -> none  [the longest x7 3.48 us: extended(): head = lax.slice_in_dim(cells, 0, width, axis=dim)]
  transfers between devices with their start and end apart: 20 -> 0, of which waited for: 11 -> 0; matrix products, arithmetic and copies ran while one was open for 7% -> 0% of each run, Pallas kernels for 0% -> 0%
where the time goes in v1:
time: 133 us
  Pallas kernels  132 us (99%)
    pallas_call x1, Pallas kernels, local(): pl.pallas_call(main_kernel, out_shape=jax.ShapeDtypeStruct((RC, 8, X), F3...  119 us
    pallas_call x1, Pallas kernels, local(): pl.pallas_call(final_kernel, out_shape=jax.ShapeDtypeStruct(iterate.shape...  12.9 us

profile of v1, /device:TPU:121, one launch (start us, length us, event | category | flops | bytes accessed | tf_op | source)
XLA Modules:
  0.0 132.7 jit_solution(14267364803196454459)
XLA Ops:
  0.0 0.0 copy-start
  0.0 118.8 %shard_map.37.e = f32[16,8,512]{2,1,0:T(8,128)} custom-call(f32[4,256,512]{2,1,0:T(8,128)} %ini.1, f32[1,4,256,512]{3,2,1,0:T(8,128)} %itr.3, f32[4,256,512]{2,1,0:T(8,128)} %dif.1), custom_call_target="tpu_custom_call" | custom-call | tf_op jit(solution)/shard_map/pallas_call | solution.py:733
  118.8 0.0 copy-done
  118.9 0.0 copy-start.1
  118.9 0.9 copy-done.1
  119.8 12.9 %shard_map.38 = f32[1,4,256,512]{3,2,1,0:T(8,128)} custom-call(f32[1,4,256,512]{3,2,1,0:T(8,128)S(1)} %copy-done, f32[16,8,512]{2,1,0:T(8,128)S(1)} %copy-done.1), custom_call_target="tpu_custom_call" | custom-call | tf_op jit(solution)/shard_map/pallas_call | solution.py:789
Async XLA Ops:
  0.0 118.8 %copy-start = (f32[1,4,256,512]{3,2,1,0:T(8,128)S(1)}, f32[1,4,256,512]{3,2,1,0:T(8,128)}, u32[]{:S(2)}) copy-start(f32[1,4,256,512]{3,2,1,0:T(8,128)} %itr.3) | copy-start | bytes 6291460
  118.9 1.0 copy-start.1

commit v2 on v1

v2 whole, which is shorter than its diff:
```python
import jax
import jax.numpy as jnp
from jax import lax
from jax.experimental import pallas as pl
from jax.experimental.pallas import tpu as pltpu
from jax.sharding import PartitionSpec as P

STEPS = 4
courant = 0.15
K = 0.5 * courant
F32 = jnp.float32
MESH = pl.DeviceIdType.MESH

Y, X = 256, 512
LT = X // 128
R = 32
RC = 16
CH = 12
PART = 8


def lane():
    return lax.broadcasted_iota(jnp.int32, (8, 128), 1)


def even():
    return (lane() & 1) == 0


def subs(shape):
    return lax.broadcasted_iota(jnp.int32, shape, 0)


def from_below(v):
    return jnp.where(subs(v.shape) == 7, 0.0, pltpu.roll(v, 7, axis=0))


def from_above(v):
    return jnp.where(subs(v.shape) == 0, 0.0, pltpu.roll(v, 1, axis=0))


def row(ref, *at):
    return [ref[(*at, slice(None), slice(128 * q, 128 * q + 128))] for q in range(LT)]


def put(ref, value, *at):
    for q in range(LT):
        ref[(*at, slice(None), slice(128 * q, 128 * q + 128))] = value[q]


def each(f, *rows):
    return [f(*t) for t in zip(*rows)]


def add(a, b):
    return each(lambda x, y: x + y, a, b)


def sub(a, b):
    return each(lambda x, y: x - y, a, b)


def mul(a, b):
    return each(lambda x, y: x * y, a, b)


def at_right(v, by=1):
    turned = [pltpu.roll(x, 128 - by, axis=1) for x in v] + [jnp.zeros((8, 128), F32)]
    return [jnp.where(lane() >= 128 - by, turned[q + 1], turned[q]) for q in range(LT)]


def at_left(v, by=1, first=None):
    turned = [jnp.zeros((8, 128), F32) if first is None else first] + [pltpu.roll(x, by, axis=1) for x in v]
    return [jnp.where(lane() < by, turned[q], turned[q + 1]) for q in range(LT)]


def swap_pairs(v):
    return [jnp.where(even(), pltpu.roll(x, 127, axis=1), pltpu.roll(x, 1, axis=1)) for x in v]


def pack(a, b):
    return each(
        lambda x, y: jnp.where(even(), x + pltpu.roll(x, 127, axis=1), y + pltpu.roll(y, 1, axis=1)), a, b
    )


def coarse_advance(c, c_up, c_dn, c_io, v, v_up, v_dn, v_io):
    flux = None
    for cn, vn in (
        (at_right(c, 2), at_right(v, 2)),
        (at_left(c, 2), at_left(v, 2)),
        (c_up, v_up),
        (c_dn, v_dn),
        (swap_pairs(c), swap_pairs(v)),
        (c_io, v_io),
    ):
        term = mul(add(c, cn), sub(vn, v))
        flux = term if flux is None else add(flux, term)
    return each(lambda x, f: x + K * f, v, flux)


def main_kernel(
    ini,
    itr,
    dif,
    out,
    cbuf,
    kx,
    ky,
    kz,
    kl,
    wa,
    wb,
    inn,
    cc,
    ccp,
    icoarse,
    ipart,
    own,
    ext,
    ccb,
    cco,
    go,
    gx,
    eb,
    hlo,
    hhi,
    hp,
    hn,
    eout,
    ld_sem,
    icp,
    chs,
    chr_,
    ins,
    inr,
    pps,
    ppr,
    cbs,
    cbr,
    cor,
    gos,
    gor,
    gxs,
    gxr,
    hs,
    hr,
    eos,
    eor,
):
    t = lax.axis_index("tm")
    s = lax.axis_index("space")
    core = s % 2
    zhi = (s // 2) % 2
    col = s // 4
    z = zhi * 4 + t
    ncol = lax.axis_size("space") // 4
    partner = s + 1 - 2 * core
    cross_ok = jnp.logical_and(
        jnp.logical_or(core == 1, s > 0), jnp.logical_or(core == 0, s < 4 * ncol - 1)
    )
    cross = jnp.where(cross_ok, s - 1 + 2 * core, s)
    qcol = cross // 4
    qzhi = (cross // 2) % 2
    qcore = cross % 2

    states = (wa, wb)

    def plane(p):
        return (3 - p) + core * (2 * p - 3)

    def dev(tt, ss):
        return {"tm": tt, "space": ss}

    barrier = pltpu.get_barrier_semaphore()

    @pl.loop(0, 16)
    def _(i):
        ti, si = i % 4, col * 4 + i // 4

        @pl.when(jnp.logical_not(jnp.logical_and(ti == t, si == s)))
        def _():
            pl.semaphore_signal(barrier, inc=1, device_id=dev(ti, si), device_id_type=MESH)

    lat_ok = jnp.logical_or(
        jnp.logical_and(core == 0, col > 0), jnp.logical_and(core == 1, col < ncol - 1)
    )
    lat_col = jnp.where(core == 0, col - 1, col + 1)

    @pl.when(lat_ok)
    def _():
        @pl.loop(0, 8)
        def _(i):
            si = lat_col * 4 + (i // 4) * 2 + 1 - core
            pl.semaphore_signal(barrier, inc=1, device_id=dev(i % 4, si), device_id_type=MESH)

    def load_rows(src, dst, sem):
        @pl.loop(0, 4)
        def _(p):
            for sl in range(8):
                pltpu.make_async_copy(
                    src.at[plane(p), pl.ds(R * sl, R), :], dst.at[p, pl.ds(1, R), sl, :], sem
                ).start()

    load_rows(dif, cbuf, ld_sem.at[0])

    @pl.when(t == 3)
    def _():
        load_rows(ini, wa, ld_sem.at[1])

    @pl.when(t != 3)
    def _():
        load_rows(itr.at[0], wa, ld_sem.at[1])

    held_c = cbuf.at[pl.ds(0, 4), pl.ds(1, R)]
    pltpu.make_async_copy(held_c, held_c, ld_sem.at[0]).wait()

    pl.semaphore_wait(barrier, jnp.where(lat_ok, 23, 15))

    def inner_c():
        return pltpu.make_async_remote_copy(
            src_ref=cbuf.at[0, pl.ds(1, R)],
            dst_ref=cbuf.at[7, pl.ds(1, R)],
            send_sem=icp.at[0],
            recv_sem=icp.at[1],
            device_id=dev(t, partner),
            device_id_type=MESH,
        )

    inner_c().start()

    def piece(j, ch, i):
        return cbuf.at[j, pl.ds(1 + (R // 2) * ch + (i % 4) * (R // 8), R // 8)]

    def first(ch, i):
        j = i // 4
        return pltpu.make_async_remote_copy(
            src_ref=piece(3 - j, ch, i),
            dst_ref=piece(4 + j, ch, i),
            send_sem=chs.at[2 + ch, i],
            recv_sem=chr_.at[ch, i],
            device_id=dev(3 - 3 * ch, cross),
            device_id_type=MESH,
        )

    def relay(ch, i):
        ref = piece(4 + i // 4, ch, i)
        return pltpu.make_async_remote_copy(
            src_ref=ref,
            dst_ref=ref,
            send_sem=chs.at[ch, i],
            recv_sem=chr_.at[ch, i],
            device_id=dev(jnp.clip(t - 1 + 2 * ch, 0, 3), s),
            device_id_type=MESH,
        )

    starts = (t == 0, t == 3)
    sends_on = (t > 0, t < 3)

    @pl.when(cross_ok)
    def _():
        for ch in range(2):

            @pl.when(starts[ch])
            def _():
                @pl.loop(0, CH)
                def _(i):
                    first(ch, i).start()

    def edge_rows(dst, d):
        dst[d, 0] = from_above(dst[d, R])
        dst[d, R + 1] = from_below(dst[d, 1])

    held_u = wa.at[pl.ds(0, 4), pl.ds(1, R)]
    pltpu.make_async_copy(held_u, held_u, ld_sem.at[1]).wait()

    def inner_state(k):
        return pltpu.make_async_remote_copy(
            src_ref=states[k % 2].at[0, pl.ds(1, R)],
            dst_ref=inn.at[k],
            send_sem=ins.at[k],
            recv_sem=inr.at[k],
            device_id=dev(t, partner),
            device_id_type=MESH,
        )

    inner_state(0).start()
    for p in range(4):
        edge_rows(wa, p)
        edge_rows(cbuf, p)

    def to_partner(i):
        src, dst = ((cc, ccp), (icoarse, ipart))[i]
        return pltpu.make_async_remote_copy(
            src_ref=src,
            dst_ref=dst,
            send_sem=pps.at[i],
            recv_sem=ppr.at[i],
            device_id=dev(t, partner),
            device_id_type=MESH,
        )

    def cross_send(is_self, src, dst, ssem, rsem, to):
        @pl.when(is_self)
        def _():
            pltpu.make_async_copy(src, dst, rsem).start()

        @pl.when(jnp.logical_not(is_self))
        def _():
            pltpu.make_async_remote_copy(
                src_ref=src,
                dst_ref=dst,
                send_sem=ssem,
                recv_sem=rsem,
                device_id=to,
                device_id_type=MESH,
            ).start()

    def cross_sent(is_self, src, dst, ssem, rsem, to):
        @pl.when(jnp.logical_not(is_self))
        def _():
            pltpu.make_async_remote_copy(
                src_ref=src,
                dst_ref=dst,
                send_sem=ssem,
                recv_sem=rsem,
                device_id=to,
                device_id_type=MESH,
            ).wait_send()

    def cc_own(h, m):
        e = t + 4 * h
        sp = col * 4 + h * 2 + zhi
        row = (2 * e - 1 + m + RC) % RC
        return sp == s, cc.at[row], ccb.at[core, m], cbs.at[h, m], cbr.at[0], dev(t, sp)

    def cc_out(h):
        e = t + 4 * h
        sp = qcol * 4 + h * 2 + qzhi
        return sp == s, cc.at[pl.ds(2 * e, 2)], cco.at[qcore], cbs.at[h, 4], cor.at[qcore], dev(t, sp)

    vflag = jnp.where(cross_ok, 1.0, 0.0).astype(F32)

    def coefficients(p):
        @pl.loop(0, R, unroll=4)
        def _(r):
            c = row(cbuf, p, r + 1)
            face = lambda n: each(lambda x, y: K * (x + y), c, n)
            put(kx, face(at_right(c)), p, r)
            put(ky, face(row(cbuf, p, r)), p, r)
            put(kz, face(row(cbuf, (p + 7) % 8, r + 1)), p, r)
            kl[p, r] = K * c[0]

        ky[p, R] = K * (cbuf[p, R] + cbuf[p, R + 1])

    def flux(coeff, a, b):
        return mul(coeff, sub(a, b))

    def step_inner(k):
        inner_state(k).wait_recv()
        src, dst = states[k % 2], states[(k + 1) % 2]
        if k > 0:
            inner_state(k - 1).wait_send()
        step_planes(k, src, dst, 0, 0)
        edge_rows(dst, 0)
        inner_state(k + 1).start()

    def step_rest(k, first, last):
        src, dst = states[k % 2], states[(k + 1) % 2]
        step_planes(k, src, dst, first, last)
        for p in range(first, last + 1 + (last == 3 + k)):
            edge_rows(dst, p)

    def step_planes(k, src, dst, first, last):
        top = 3 + k

        @pl.loop(0, R // 2, unroll=2)
        def _(i):
            r = 2 * i
            below = [row(inn, k, r + j) if first == 0 else row(src, first - 1, r + j + 1) for j in range(2)]
            v = [row(src, first, r + j + 1) for j in range(2)]
            fz = [flux(row(kz, first, r + j), v[j], below[j]) for j in range(2)]
            for p in range(first, last + 1):
                above = None
                if p < top:
                    above = [row(src, p + 1, r + j + 1) for j in range(2)]
                around = [row(src, p, r)] + v + [row(src, p, r + 3)]
                fy = [flux(row(ky, p, r + j), around[j + 1], around[j]) for j in range(3)]
                fz_next = []
                for j in range(2):
                    fx = flux(row(kx, p, r + j), at_right(v[j]), v[j])
                    total = sub(fx, at_left(fx, 1, kl[p, r + j] * v[j][0]))
                    total = add(total, sub(fy[j + 1], fy[j]))
                    if above is None:
                        out_flow = mul(row(kz, p + 1, r + j), v[j])
                        total = sub(total, add(out_flow, fz[j]))
                        if top == 3:
                            out_flow = [vflag * x for x in out_flow]
                        put(dst, out_flow, p + 1, r + j + 1)
                    else:
                        fz_next.append(flux(row(kz, p + 1, r + j), above[j], v[j]))
                        total = add(total, sub(fz_next[j], fz[j]))
                    new = add(v[j], total)
                    if p == 4:
                        new = [vflag * x for x in new]
                    put(dst, new, p, r + j + 1)
                v, fz = above, fz_next

    def restricted():
        @pl.loop(0, RC, unroll=2)
        def _(r):
            def block(src, p):
                a = 2 * r + 1
                return add(add(row(src, p, a), row(src, p, a + 1)), add(row(src, p + 1, a), row(src, p + 1, a + 1)))

            put(cc, [0.125 * x for x in pack(block(cbuf, 0), block(cbuf, 2))], r)
            put(icoarse, [0.125 * x for x in pack(block(wa, 0), block(wa, 2))], r)

    def own_first():
        inner_c().wait_recv()
        edge_rows(cbuf, 7)
        coefficients(0)

    def share_coarse():
        to_partner(0).start()
        to_partner(1).start()
        for h in range(2):
            for m in range(4):
                cross_send(*cc_own(h, m))

            @pl.when(cross_ok)
            def _():
                cross_send(*cc_out(h))

    def after_plane(p, then=None):
        edge_rows(cbuf, p)
        coefficients(p)
        if then is not None:
            then(p - 4)

    early = (restricted, own_first, lambda: coefficients(1), lambda: coefficients(2), lambda: coefficients(3))
    late = (
        lambda: after_plane(4),
        lambda: step_inner(0),
        lambda: step_rest(0, 1, 3),
        share_coarse,
        lambda: after_plane(5, step_inner),
        lambda: step_rest(1, 1, 4),
        lambda: step_inner(2),
        lambda: step_rest(2, 1, 4),
    )

    off = tuple(
        jnp.where(t == last, 7, jnp.where(t == near, 3, 0)) for last, near in ((0, 1), (3, 2))
    )
    off_max = jnp.maximum(off[0], off[1])

    @pl.when(jnp.logical_not(cross_ok))
    def _():
        for p in range(4, 7):

            @pl.loop(0, R + 2)
            def _(r):
                cbuf[p, r] = jnp.zeros((8, X), F32)

    @pl.loop(0, CH + 7)
    def _(n):
        for ch in range(2):
            i = n - off[ch]

            @pl.when(jnp.logical_and(cross_ok, jnp.logical_and(i >= 0, i < CH)))
            def _():
                relay(ch, i).wait_recv()

                @pl.when(sends_on[ch])
                def _():
                    relay(ch, i).start()

        for m, work in enumerate(early):
            pl.when(n == m)(work)
        for m, work in enumerate(late):
            pl.when(n == 3 + off_max + m)(work)

    to_partner(0).wait_recv()
    to_partner(1).wait_recv()
    gflag = jnp.where(t == 3, 0.0, 1.0).astype(F32)
    inner_state(STEPS - 1).wait_recv()

    def last_groups(r, groups, low):
        src = states[(STEPS - 1) % 2]
        ends = []
        v = [row(src, groups[0][0], r + j + 1) for j in range(2)]
        low = [flux(row(kz, groups[0][0], r + j), v[j], low(j)) for j in range(2)]
        low = add(low[0], low[1])
        for planes in groups:
            held = fxs = net = kls = None
            for p in planes:
                fy = sub(
                    flux(row(ky, p, r + 2), row(src, p, r + 3), v[1]), flux(row(ky, p, r), v[0], row(src, p, r))
                )
                net = fy if net is None else add(net, fy)
                for j in range(2):
                    fx = flux(row(kx, p, r + j), at_right(v[j]), v[j])
                    fl = kl[p, r + j] * v[j][0]
                    fxs = fx if fxs is None else add(fxs, fx)
                    kls = fl if kls is None else kls + fl
                both = add(v[0], v[1])
                held = both if held is None else add(held, both)
                if p < 6:
                    last_v, v = v, [row(src, p + 1, r + j + 1) for j in range(2)]
            net = sub(net, low)
            if planes[-1] < 6:
                high = [flux(row(kz, planes[-1] + 1, r + j), v[j], last_v[j]) for j in range(2)]
                low = add(high[0], high[1])
                net = add(net, low)
            held = add(held, net)
            right = [pltpu.roll(x, 127, axis=1) for x in add(held, fxs)]
            ends.append(sub(add(held, right), at_left(fxs, 1, kls)))
        return ends

    def packed(a, b):
        return each(lambda x, y: 0.125 * jnp.where(even(), x, pltpu.roll(y, 1, axis=1)), a, b)

    def coarse_side(rc):
        a = 2 * rc + 1
        outer = add(add(row(cbuf, 4, a), row(cbuf, 4, a + 1)), add(row(cbuf, 5, a), row(cbuf, 5, a + 1)))
        return each(lambda x, y: jnp.where(even(), x, 0.125 * y), row(ccp, rc), pack(outer, outer))

    def own_row(rc):
        lo = jnp.maximum(rc - 1, 0)
        hi = jnp.minimum(rc + 1, RC - 1)

        def neighbours(ref):
            up = each(lambda x, y: jnp.where(rc == RC - 1, from_below(y), x), row(ref, hi), row(ref, 0))
            dn = each(lambda x, y: jnp.where(rc == 0, from_above(y), x), row(ref, lo), row(ref, RC - 1))
            return up, dn

        ends = last_groups(2 * rc, ((0, 1), (2, 3)), lambda j: row(inn, STEPS - 1, 2 * rc + j))
        c_up, c_dn = neighbours(cc)
        u_up, u_dn = neighbours(icoarse)
        u_io = [jnp.where(even(), x, 0.0) for x in row(ipart, rc)]
        back = coarse_advance(
            row(cc, rc), c_up, c_dn, coarse_side(rc), row(icoarse, rc), u_up, u_dn, u_io
        )
        put(own, each(lambda x, y: x - gflag * y, packed(ends[0], ends[1]), back), rc)

    def ext_row(rc):
        src = states[(STEPS - 1) % 2]
        ends = last_groups(2 * rc, ((4, 5), (6,)), lambda j: row(src, 3, 2 * rc + j + 1))
        lost = each(
            lambda x, y, z: jnp.where(even(), 0.0, K * (x + y) * z),
            row(cc, rc),
            coarse_side(rc),
            row(icoarse, rc),
        )
        put(ext, each(lambda x, y: x - gflag * y, packed(ends[1], ends[0]), lost), rc)

    def o_send(e):
        sp = col * 4 + (e // 4) * 2 + zhi
        te = e % 4
        return (
            jnp.logical_and(sp == s, te == t),
            own.at[pl.ds(2 * e, 2)],
            go.at[t, core],
            gos.at[e],
            gor.at[0],
            dev(te, sp),
        )

    def x_send(e):
        sp = qcol * 4 + (e // 4) * 2 + qzhi
        te = e % 4
        return (
            jnp.logical_and(sp == s, te == t),
            ext.at[pl.ds(2 * e, 2)],
            gx.at[qcore, t],
            gxs.at[e],
            gxr.at[qcore],
            dev(te, sp),
        )

    def rows_and_sends(one_row, send):
        @pl.loop(0, 9)
        def _(i):
            @pl.when(i < 8)
            def _():
                e = (z + 4 + i) % 8
                one_row(2 * e)
                one_row(2 * e + 1)

            @pl.when(i > 0)
            def _():
                cross_send(*send((z + 3 + i) % 8))

    rows_and_sends(own_row, o_send)
    after_plane(6)
    step_rest(2, 5, 5)

    @pl.when(cross_ok)
    def _():
        rows_and_sends(ext_row, x_send)

    prev_ok = jnp.logical_or(core == 1, col > 0)
    next_ok = jnp.logical_or(core == 0, col < ncol - 1)
    prev_sp = jnp.where(core == 1, s - 1, jnp.maximum(col - 1, 0) * 4 + zhi * 2 + 1)
    next_sp = jnp.where(core == 0, s + 1, jnp.minimum(col + 1, ncol - 1) * 4 + zhi * 2)
    side_ok = (prev_ok, next_ok)

    pltpu.make_async_copy(ccb, ccb, cbr.at[0]).wait()
    for j in range(2):

        @pl.when(side_ok[j])
        def _():
            pltpu.make_async_copy(cco.at[j], cco.at[j], cor.at[j]).wait()

        @pl.when(jnp.logical_not(side_ok[j]))
        def _():
            cco[j] = jnp.zeros((2, 8, X), F32)
            gx[j] = jnp.zeros((4, 2, 8, X), F32)

    pltpu.make_async_copy(go, go, gor.at[0]).wait()
    for j in range(2):

        @pl.when(side_ok[j])
        def _():
            pltpu.make_async_copy(gx.at[j], gx.at[j], gxr.at[j]).wait()

    zu, zd = (z + 1) % 8, (z + 7) % 8

    def e_halo(k, kind):
        if kind == 0:
            src, dst, to = eb.at[k, 0], hhi.at[k], dev(zd % 4, col * 4 + (zd // 4) * 2 + core)
        elif kind == 1:
            src, dst, to = eb.at[k, 1], hlo.at[k], dev(zu % 4, col * 4 + (zu // 4) * 2 + core)
        elif kind == 2:
            src, dst, to = eb.at[k, :, 0], hn.at[k], dev(t, prev_sp)
        else:
            src, dst, to = eb.at[k, :, 1], hp.at[k], dev(t, next_sp)
        return pltpu.make_async_remote_copy(
            src_ref=src,
            dst_ref=dst,
            send_sem=hs.at[k, kind],
            recv_sem=hr.at[k, kind],
            device_id=to,
            device_id_type=MESH,
        )

    def e_back(k, j):
        sp = col * 4 + core * 2 + j
        return (
            jnp.logical_and(sp == s, t == k),
            eb.at[k, :, j],
            eout.at[pl.ds(2 * z, 2)],
            eos.at[k, j],
            eor.at[0],
            dev(k, sp),
        )

    for b in range(2):
        for j in range(2):
            eb[0, b, j] = go[3, j, b] + gx[j, 3, b]

    def send_level(k):
        if k < 3:
            e_halo(k, 0).start()
            e_halo(k, 1).start()

            @pl.when(prev_ok)
            def _():
                e_halo(k, 2).start()

            @pl.when(next_ok)
            def _():
                e_halo(k, 3).start()

        for j in range(2):
            cross_send(*e_back(k, j))

    send_level(0)
    for k in range(3):
        e_halo(k, 0).wait_recv()
        e_halo(k, 1).wait_recv()

        @pl.when(next_ok)
        def _():
            e_halo(k, 2).wait_recv()

        @pl.when(prev_ok)
        def _():
            e_halo(k, 3).wait_recv()

        @pl.when(jnp.logical_not(next_ok))
        def _():
            hn[k] = jnp.zeros((2, 8, X), F32)

        @pl.when(jnp.logical_not(prev_ok))
        def _():
            hp[k] = jnp.zeros((2, 8, X), F32)

        for j in range(2):

            def wrapped(x, c, turn, at_end):
                return [jnp.where(at_end, turn(y), y) for y in row(x, *c)]

            vs = (
                wrapped(hlo, (k, j), from_above, z == 0),
                row(eb, k, 0, j),
                row(eb, k, 1, j),
                wrapped(hhi, (k, j), from_below, z == 7),
            )
            cs = (
                wrapped(ccb, (j, 0), from_above, z == 0),
                row(ccb, j, 1),
                row(ccb, j, 2),
                wrapped(ccb, (j, 3), from_below, z == 7),
            )
            for b in range(2):
                far = row(hp if j == 0 else hn, k, b)
                v_io = each(lambda x, y: jnp.where(even(), x, y), row(eb, k, b, 1 - j), far)
                c_io = each(lambda x, y: jnp.where(even(), x, y), row(ccb, 1 - j, b + 1), row(cco, j, b))
                new = coarse_advance(
                    cs[b + 1], cs[b + 2], cs[b], c_io, vs[b + 1], vs[b + 2], vs[b], v_io
                )
                put(eb, add(new, add(row(go, k, j, b), row(gx, j, k, b))), k + 1, b, j)
        send_level(k + 1)

    pltpu.make_async_copy(eout, eout, eor.at[0]).wait()
    result = pltpu.make_async_copy(eout, out, ld_sem.at[0])
    result.start()

    inner_c().wait_send()
    for k in range(STEPS - 2, STEPS):
        inner_state(k).wait_send()
    for i in range(2):
        to_partner(i).wait_send()

    @pl.when(cross_ok)
    def _():
        for ch in range(2):

            @pl.when(starts[ch])
            def _():
                @pl.loop(0, CH)
                def _(i):
                    first(ch, i).wait_send()

            @pl.when(sends_on[ch])
            def _():
                @pl.loop(0, CH)
                def _(i):
                    relay(ch, i).wait_send()

    for h in range(2):
        for m in range(4):
            cross_sent(*cc_own(h, m))

        @pl.when(cross_ok)
        def _():
            cross_sent(*cc_out(h))

    @pl.loop(0, 8)
    def _(e):
        cross_sent(*o_send(e))

        @pl.when(cross_ok)
        def _():
            cross_sent(*x_send(e))

    for k in range(3):
        e_halo(k, 0).wait_send()
        e_halo(k, 1).wait_send()

        @pl.when(prev_ok)
        def _():
            e_halo(k, 2).wait_send()

        @pl.when(next_ok)
        def _():
            e_halo(k, 3).wait_send()

    for k in range(4):
        for j in range(2):
            cross_sent(*e_back(k, j))
    result.wait()


def final_kernel(itr, err, out, e, raw, res, esem, isem, osem):
    core = lax.axis_index("space") % 2

    def plane(p):
        return (3 - p) + core * (2 * p - 3)

    def load(n, sl):
        return pltpu.make_async_copy(
            itr.at[0, :, pl.ds(R * sl + PART * n, PART), :], raw.at[n, :, :, sl, :], isem.at[n]
        )

    def store(n, sl):
        return pltpu.make_async_copy(
            res.at[n, :, :, sl, :], out.at[0, :, pl.ds(R * sl + PART * n, PART), :], osem.at[n]
        )

    fetch = pltpu.make_async_copy(err, e, esem.at[0])
    fetch.start()
    for n in range(R // PART):
        for sl in range(8):
            load(n, sl).start()
    fetch.wait()
    for n in range(R // PART):
        pltpu.make_async_copy(raw.at[n], raw.at[n], isem.at[n]).wait()

        @pl.loop(0, PART // 2, unroll=2)
        def _(r):
            rows = [[row(raw, n, plane(p), 2 * r + b) for b in range(2)] for p in range(4)]
            a = add(add(*rows[0]), add(*rows[1]))
            c = add(add(*rows[2]), add(*rows[3]))
            d = each(lambda x, y: x - 0.125 * y, row(e, (PART // 2) * n + r), pack(a, c))
            halves = (
                [jnp.where(even(), x, pltpu.roll(x, 1, axis=1)) for x in d],
                [jnp.where(even(), pltpu.roll(x, 127, axis=1), x) for x in d],
            )
            for p in range(4):
                for b in range(2):
                    put(res, add(rows[p][b], halves[p // 2]), n, plane(p), 2 * r + b)

        for sl in range(8):
            store(n, sl).start()
    for n in range(R // PART):
        pltpu.make_async_copy(res.at[n], res.at[n], osem.at[n]).wait()


def local(initial, iterate, diffusivity):
    vm = lambda *shape: pltpu.VMEM(shape, F32)
    dma = lambda *shape: pltpu.SemaphoreType.DMA(shape)
    hbm = pl.BlockSpec(memory_space=pl.ANY)
    err = pl.pallas_call(
        main_kernel,
        out_shape=jax.ShapeDtypeStruct((RC, 8, X), F32),
        in_specs=[hbm] * 3,
        out_specs=hbm,
        scratch_shapes=[
            vm(8, R + 2, 8, X),
            vm(7, R, 8, X),
            vm(7, R + 1, 8, X),
            vm(7, R, 8, X),
            vm(7, R, 8, 128),
            vm(7, R + 2, 8, X),
            vm(7, R + 2, 8, X),
            vm(STEPS, R, 8, X),
            vm(RC, 8, X),
            vm(RC, 8, X),
            vm(RC, 8, X),
            vm(RC, 8, X),
            vm(RC, 8, X),
            vm(RC, 8, X),
            vm(2, 4, 8, X),
            vm(2, 2, 8, X),
            vm(4, 2, 2, 8, X),
            vm(2, 4, 2, 8, X),
            vm(4, 2, 2, 8, X),
            vm(3, 2, 8, X),
            vm(3, 2, 8, X),
            vm(3, 2, 8, X),
            vm(3, 2, 8, X),
            vm(RC, 8, X),
            dma(2),
            dma(2),
            dma(4, CH),
            dma(2, CH),
            dma(STEPS),
            dma(STEPS),
            dma(2),
            dma(2),
            dma(2, 5),
            dma(1),
            dma(2),
            dma(8),
            dma(1),
            dma(8),
            dma(2),
            dma(3, 4),
            dma(3, 4),
            dma(4, 2),
            dma(1),
        ],
        compiler_params=pltpu.CompilerParams(
            collective_id=0, has_side_effects=True, vmem_limit_bytes=60 * 2**20
        ),
    )(initial, iterate, diffusivity)
    return pl.pallas_call(
        final_kernel,
        out_shape=jax.ShapeDtypeStruct(iterate.shape, F32),
        in_specs=[hbm, hbm],
        out_specs=hbm,
        scratch_shapes=[
            vm(RC, 8, X),
            vm(R // PART, 4, PART, 8, X),
            vm(R // PART, 4, PART, 8, X),
            dma(1),
            dma(R // PART),
            dma(R // PART),
        ],
        compiler_params=pltpu.CompilerParams(vmem_limit_bytes=16 * 2**20),
    )(iterate, err)


def solution(mesh):
    placed = (P("space", None, None), P("tm", "space", None, None), P("space", None, None))
    return jax.shard_map(
        local, mesh=mesh, in_specs=placed, out_specs=P("tm", "space", None, None), check_vma=False
    )
```

time: 133 us -> 84.7 us (0.64)
  Pallas kernels: 132 us -> 83.6 us
    pallas_call x1, Pallas kernels: 119 us -> 79.8 us  [local(): pl.pallas_call(main_kernel, out_shape=jax.ShapeDtypeStruct((RC, 8, X), F3...]
    pallas_call x1, Pallas kernels: 12.9 us -> 3.86 us  [local(): pl.pallas_call(final_kernel, out_shape=jax.ShapeDtypeStruct(iterate.shape...]
where the time goes in v2:
time: 84.7 us; the launch traced here: 84.6 us
  Pallas kernels  83.6 us (99%)
  local copies, waits for them, and re-layouts  0.95 us (1%)
    pallas_call x1, Pallas kernels, local(): pl.pallas_call(main_kernel, out_shape=jax.ShapeDtypeStruct((RC, 8, X), F3...  79.8 us
    pallas_call x1, Pallas kernels, local(): pl.pallas_call(final_kernel, out_shape=jax.ShapeDtypeStruct(iterate.shape...  3.86 us

profile of v2, /device:TPU:121, one launch (start us, length us, event | category | flops | bytes accessed | tf_op | source)
XLA Modules:
  0.0 84.6 jit_solution(6532124733899343122)
XLA Ops:
  0.0 0.0 copy-start
  0.0 79.8 %shard_map.37.err = f32[16,8,512]{2,1,0:T(8,128)} custom-call(f32[4,256,512]{2,1,0:T(8,128)} %ini.1, f32[1,4,256,512]{3,2,1,0:T(8,128)} %itr.3, f32[4,256,512]{2,1,0:T(8,128)} %dif.1), custom_call_target="tpu_custom_call" | custom-call | tf_op jit(solution)/shard_map/pallas_call | solution.py:836
  79.8 0.0 copy-done
  79.8 0.0 copy-start.1
  79.8 0.9 %copy-done.1 = f32[16,8,512]{2,1,0:T(8,128)S(1)} copy-done((f32[16,8,512]{2,1,0:T(8,128)S(1)}, f32[16,8,512]{2,1,0:T(8,128)}, u32[]{:S(2)}) %copy-start.1) | copy-done | bytes 262168
  80.8 3.9 %shard_map.38 = f32[1,4,256,512]{3,2,1,0:T(8,128)} custom-call(f32[1,4,256,512]{3,2,1,0:T(8,128)S(1)} %copy-done, f32[16,8,512]{2,1,0:T(8,128)S(1)} %copy-done.1), custom_call_target="tpu_custom_call" | custom-call | tf_op jit(solution)/shard_map/pallas_call | solution.py:890
Async XLA Ops:
  0.0 79.8 %copy-start = (f32[1,4,256,512]{3,2,1,0:T(8,128)S(1)}, f32[1,4,256,512]{3,2,1,0:T(8,128)}, u32[]{:S(2)}) copy-start(f32[1,4,256,512]{3,2,1,0:T(8,128)} %itr.3) | copy-start | bytes 6291460
  79.8 1.0 %copy-start.1 = (f32[16,8,512]{2,1,0:T(8,128)S(1)}, f32[16,8,512]{2,1,0:T(8,128)}, u32[]{:S(2)}) copy-start(f32[16,8,512]{2,1,0:T(8,128)} %shard_map.37.err) | copy-start | bytes 786436

commit v3 on v2

--- a/solution.py
+++ b/solution.py
@@ -1,3 +1,5 @@
+import functools
+
 import jax
 import jax.numpy as jnp
 from jax import lax
@@ -15,8 +17,12 @@
 LT = X // 128
 R = 32
 RC = 16
-CH = 12
-PART = 8
+CH = 24
+LEAD, FAR = 5, 14
+PART = 64
+
+
+PER = CH // 3
 
 
 def lane():
@@ -128,6 +134,7 @@
     hp,
     hn,
     eout,
+    wide,
     ld_sem,
     icp,
     chs,
@@ -138,6 +145,7 @@
     ppr,
     cbs,
     cbr,
+    cos,
     cor,
     gos,
     gor,
@@ -230,10 +238,10 @@
     inner_c().start()
 
     def piece(j, ch, i):
-        return cbuf.at[j, pl.ds(1 + (R // 2) * ch + (i % 4) * (R // 8), R // 8)]
+        return cbuf.at[j, pl.ds(1 + (R // 2) * ch + (i % PER) * (R // 2 // PER), R // 2 // PER)]
 
     def first(ch, i):
-        j = i // 4
+        j = i // PER
         return pltpu.make_async_remote_copy(
             src_ref=piece(3 - j, ch, i),
             dst_ref=piece(4 + j, ch, i),
@@ -244,7 +252,7 @@
         )
 
     def relay(ch, i):
-        ref = piece(4 + i // 4, ch, i)
+        ref = piece(4 + i // PER, ch, i)
         return pltpu.make_async_remote_copy(
             src_ref=ref,
             dst_ref=ref,
@@ -328,18 +336,64 @@
                 device_id_type=MESH,
             ).wait_send()
 
-    def cc_own(h, m):
+    def cc_own(h):
         e = t + 4 * h
         sp = col * 4 + h * 2 + zhi
-        row = (2 * e - 1 + m + RC) % RC
-        return sp == s, cc.at[row], ccb.at[core, m], cbs.at[h, m], cbr.at[0], dev(t, sp)
-
-    def cc_out(h):
-        e = t + 4 * h
-        sp = qcol * 4 + h * 2 + qzhi
-        return sp == s, cc.at[pl.ds(2 * e, 2)], cco.at[qcore], cbs.at[h, 4], cor.at[qcore], dev(t, sp)
+        return (
+            sp == s,
+            cc.at[pl.ds(2 * e, 2)],
+            ccb.at[core, pl.ds(1, 2)],
+            cbs.at[h],
+            cbr.at[0],
+            dev(t, sp),
+        )
+
+    prev_ok = jnp.logical_or(core == 1, col > 0)
+    next_ok = jnp.logical_or(core == 0, col < ncol - 1)
+    prev_sp = jnp.where(core == 1, s - 1, jnp.maximum(col - 1, 0) * 4 + zhi * 2 + 1)
+    next_sp = jnp.where(core == 0, s + 1, jnp.minimum(col + 1, ncol - 1) * 4 + zhi * 2)
+    side_ok = (prev_ok, next_ok)
+
+    zu, zd = (z + 1) % 8, (z + 7) % 8
+    beside = (
+        dev(zd % 4, col * 4 + (zd // 4) * 2 + core),
+        dev(zu % 4, col * 4 + (zu // 4) * 2 + core),
+        dev(t, prev_sp),
+        dev(t, next_sp),
+    )
+
+    def c_halo(kind):
+        src, dst = (
+            (ccb.at[:, 1], ccb.at[:, 3]),
+            (ccb.at[:, 2], ccb.at[:, 0]),
+            (ccb.at[0, pl.ds(1, 2)], cco.at[1]),
+            (ccb.at[1, pl.ds(1, 2)], cco.at[0]),
+        )[kind]
+        return pltpu.make_async_remote_copy(
+            src_ref=src,
+            dst_ref=dst,
+            send_sem=cos.at[kind],
+            recv_sem=cor.at[kind],
+            device_id=beside[kind],
+            device_id_type=MESH,
+        )
+
+    def share_halos():
+        held = ccb.at[:, pl.ds(1, 2)]
+        pltpu.make_async_copy(held, held, cbr.at[0]).wait()
+        c_halo(0).start()
+        c_halo(1).start()
+
+        @pl.when(prev_ok)
+        def _():
+            c_halo(2).start()
+
+        @pl.when(next_ok)
+        def _():
+            c_halo(3).start()
 
     vflag = jnp.where(cross_ok, 1.0, 0.0).astype(F32)
+    gflag = jnp.where(t == 3, 0.0, 1.0).astype(F32)
 
     def coefficients(p):
         @pl.loop(0, R, unroll=4)
@@ -356,25 +410,29 @@
     def flux(coeff, a, b):
         return mul(coeff, sub(a, b))
 
-    def step_inner(k):
-        inner_state(k).wait_recv()
+    def step_inner(k, lo=0, hi=R // 2):
         src, dst = states[k % 2], states[(k + 1) % 2]
-        if k > 0:
-            inner_state(k - 1).wait_send()
-        step_planes(k, src, dst, 0, 0)
-        edge_rows(dst, 0)
-        inner_state(k + 1).start()
-
-    def step_rest(k, first, last):
+        if lo == 0:
+            inner_state(k).wait_recv()
+            if k > 0:
+                inner_state(k - 1).wait_send()
+        step_planes(k, src, dst, 0, 0, lo, hi)
+        if hi == R // 2:
+            edge_rows(dst, 0)
+            inner_state(k + 1).start()
+
+    def step_rest(k, first, last, lo=0, hi=R // 2):
         src, dst = states[k % 2], states[(k + 1) % 2]
-        step_planes(k, src, dst, first, last)
+        step_planes(k, src, dst, first, last, lo, hi)
+        if hi < R // 2:
+            return
         for p in range(first, last + 1 + (last == 3 + k)):
             edge_rows(dst, p)
 
-    def step_planes(k, src, dst, first, last):
+    def step_planes(k, src, dst, first, last, lo, hi):
         top = 3 + k
 
-        @pl.loop(0, R // 2, unroll=2)
+        @pl.loop(lo, hi, unroll=2)
         def _(i):
             r = 2 * i
             below = [row(inn, k, r + j) if first == 0 else row(src, first - 1, r + j + 1) for j in range(2)]
@@ -425,66 +483,11 @@
         to_partner(0).start()
         to_partner(1).start()
         for h in range(2):
-            for m in range(4):
-                cross_send(*cc_own(h, m))
-
-            @pl.when(cross_ok)
-            def _():
-                cross_send(*cc_out(h))
-
-    def after_plane(p, then=None):
+            cross_send(*cc_own(h))
+
+    def after_plane(p):
         edge_rows(cbuf, p)
         coefficients(p)
-        if then is not None:
-            then(p - 4)
-
-    early = (restricted, own_first, lambda: coefficients(1), lambda: coefficients(2), lambda: coefficients(3))
-    late = (
-        lambda: after_plane(4),
-        lambda: step_inner(0),
-        lambda: step_rest(0, 1, 3),
-        share_coarse,
-        lambda: after_plane(5, step_inner),
-        lambda: step_rest(1, 1, 4),
-        lambda: step_inner(2),
-        lambda: step_rest(2, 1, 4),
-    )
-
-    off = tuple(
-        jnp.where(t == last, 7, jnp.where(t == near, 3, 0)) for last, near in ((0, 1), (3, 2))
-    )
-    off_max = jnp.maximum(off[0], off[1])
-
-    @pl.when(jnp.logical_not(cross_ok))
-    def _():
-        for p in range(4, 7):
-
-            @pl.loop(0, R + 2)
-            def _(r):
-                cbuf[p, r] = jnp.zeros((8, X), F32)
-
-    @pl.loop(0, CH + 7)
-    def _(n):
-        for ch in range(2):
-            i = n - off[ch]
-
-            @pl.when(jnp.logical_and(cross_ok, jnp.logical_and(i >= 0, i < CH)))
-            def _():
-                relay(ch, i).wait_recv()
-
-                @pl.when(sends_on[ch])
-                def _():
-                    relay(ch, i).start()
-
-        for m, work in enumerate(early):
-            pl.when(n == m)(work)
-        for m, work in enumerate(late):
-            pl.when(n == 3 + off_max + m)(work)
-
-    to_partner(0).wait_recv()
-    to_partner(1).wait_recv()
-    gflag = jnp.where(t == 3, 0.0, 1.0).astype(F32)
-    inner_state(STEPS - 1).wait_recv()
 
     def last_groups(r, groups, low):
         src = states[(STEPS - 1) % 2]
@@ -526,6 +529,14 @@
         outer = add(add(row(cbuf, 4, a), row(cbuf, 4, a + 1)), add(row(cbuf, 5, a), row(cbuf, 5, a + 1)))
         return each(lambda x, y: jnp.where(even(), x, 0.125 * y), row(ccp, rc), pack(outer, outer))
 
+    def inner_rows(lo, hi):
+        if lo == 0:
+            inner_state(STEPS - 1).wait_recv()
+
+        @pl.loop(lo, hi)
+        def _(rc):
+            put(own, last_groups(2 * rc, ((0, 1),), lambda j: row(inn, STEPS - 1, 2 * rc + j))[0], rc)
+
     def own_row(rc):
         lo = jnp.maximum(rc - 1, 0)
         hi = jnp.minimum(rc + 1, RC - 1)
@@ -535,14 +546,15 @@
             dn = each(lambda x, y: jnp.where(rc == 0, from_above(y), x), row(ref, lo), row(ref, RC - 1))
             return up, dn
 
-        ends = last_groups(2 * rc, ((0, 1), (2, 3)), lambda j: row(inn, STEPS - 1, 2 * rc + j))
+        src = states[(STEPS - 1) % 2]
+        ends = last_groups(2 * rc, ((2, 3),), lambda j: row(src, 1, 2 * rc + j + 1))
         c_up, c_dn = neighbours(cc)
         u_up, u_dn = neighbours(icoarse)
         u_io = [jnp.where(even(), x, 0.0) for x in row(ipart, rc)]
         back = coarse_advance(
             row(cc, rc), c_up, c_dn, coarse_side(rc), row(icoarse, rc), u_up, u_dn, u_io
         )
-        put(own, each(lambda x, y: x - gflag * y, packed(ends[0], ends[1]), back), rc)
+        put(own, each(lambda x, y: x - gflag * y, packed(row(own, rc), ends[0]), back), rc)
 
     def ext_row(rc):
         src = states[(STEPS - 1) % 2]
@@ -555,6 +567,79 @@
         )
         put(ext, each(lambda x, y: x - gflag * y, packed(ends[1], ends[0]), lost), rc)
 
+    def parts(f, *args, n):
+        cuts = [R // 2 * i // n for i in range(n + 1)]
+        return [functools.partial(f, *args, lo, hi) for lo, hi in zip(cuts, cuts[1:])]
+
+    first_items = [functools.partial(coefficients, p) for p in (1, 2, 3)] + parts(step_inner, 0, n=2)
+    items = [
+        *parts(step_rest, 0, 1, 2, n=4),
+        *parts(step_inner, 1, n=2),
+        *parts(step_rest, 1, 1, 1, n=2),
+        *parts(step_inner, 2, n=2),
+    ]
+    items += [None] * (PER - 1 + FAR - len(first_items) - len(items))
+    items += [
+        functools.partial(after_plane, 4),
+        *parts(step_rest, 0, 3, 3, n=2),
+        *parts(step_rest, 1, 2, 3, n=4),
+        *parts(step_rest, 2, 1, 2, n=4),
+        *parts(inner_rows, n=4),
+        functools.partial(after_plane, 5),
+        *parts(step_rest, 1, 4, 4, n=2),
+        *parts(step_rest, 2, 3, 4, n=4),
+    ]
+    middle = jnp.logical_or(t == 1, t == 2)
+    restricted()
+    share_coarse()
+    own_first()
+
+    @pl.when(middle)
+    def _():
+        for work in first_items:
+            work()
+
+    def on_ends(work):
+        return lambda: pl.when(jnp.logical_not(middle))(work)
+
+    items = [on_ends(work) for work in first_items] + items
+
+    off = tuple(
+        jnp.where(t == last, FAR, jnp.where(t == near, LEAD, 0)) for last, near in ((0, 1), (3, 2))
+    )
+
+    @pl.when(jnp.logical_not(cross_ok))
+    def _():
+        for p in range(4, 7):
+
+            @pl.loop(0, R + 2)
+            def _(r):
+                cbuf[p, r] = jnp.zeros((8, X), F32)
+
+    @pl.loop(0, max(CH + FAR, len(items)))
+    def _(n):
+        for ch in range(2):
+            i = n - off[ch]
+
+            @pl.when(jnp.logical_and(cross_ok, jnp.logical_and(i >= 0, i < CH)))
+            def _():
+                relay(ch, i).wait_recv()
+
+                @pl.when(sends_on[ch])
+                def _():
+                    relay(ch, i).start()
+
+        for group in range(0, len(items), 8):
+
+            @pl.when(jnp.logical_and(n >= group, n < group + 8))
+            def _():
+                for m, work in enumerate(items[group : group + 8]):
+                    if work is not None:
+                        pl.when(n == group + m)(work)
+
+    to_partner(0).wait_recv()
+    to_partner(1).wait_recv()
+
     def o_send(e):
         sp = col * 4 + (e // 4) * 2 + zhi
         te = e % 4
@@ -563,7 +648,7 @@
             own.at[pl.ds(2 * e, 2)],
             go.at[t, core],
             gos.at[e],
-            gor.at[0],
+            gor.at[t],
             dev(te, sp),
         )
 
@@ -575,7 +660,7 @@
             ext.at[pl.ds(2 * e, 2)],
             gx.at[qcore, t],
             gxs.at[e],
-            gxr.at[qcore],
+            gxr.at[qcore, t],
             dev(te, sp),
         )
 
@@ -592,6 +677,7 @@
             def _():
                 cross_send(*send((z + 3 + i) % 8))
 
+    share_halos()
     rows_and_sends(own_row, o_send)
     after_plane(6)
     step_rest(2, 5, 5)
@@ -600,48 +686,45 @@
     def _():
         rows_and_sends(ext_row, x_send)
 
-    prev_ok = jnp.logical_or(core == 1, col > 0)
-    next_ok = jnp.logical_or(core == 0, col < ncol - 1)
-    prev_sp = jnp.where(core == 1, s - 1, jnp.maximum(col - 1, 0) * 4 + zhi * 2 + 1)
-    next_sp = jnp.where(core == 0, s + 1, jnp.minimum(col + 1, ncol - 1) * 4 + zhi * 2)
-    side_ok = (prev_ok, next_ok)
-
-    pltpu.make_async_copy(ccb, ccb, cbr.at[0]).wait()
+    c_halo(0).wait_recv()
+    c_halo(1).wait_recv()
+
+    @pl.when(next_ok)
+    def _():
+        c_halo(2).wait_recv()
+
+    @pl.when(prev_ok)
+    def _():
+        c_halo(3).wait_recv()
+
     for j in range(2):
-
-        @pl.when(side_ok[j])
-        def _():
-            pltpu.make_async_copy(cco.at[j], cco.at[j], cor.at[j]).wait()
 
         @pl.when(jnp.logical_not(side_ok[j]))
         def _():
             cco[j] = jnp.zeros((2, 8, X), F32)
             gx[j] = jnp.zeros((4, 2, 8, X), F32)
 
-    pltpu.make_async_copy(go, go, gor.at[0]).wait()
-    for j in range(2):
-
-        @pl.when(side_ok[j])
-        def _():
-            pltpu.make_async_copy(gx.at[j], gx.at[j], gxr.at[j]).wait()
-
-    zu, zd = (z + 1) % 8, (z + 7) % 8
+    def arrived(g):
+        pltpu.make_async_copy(go.at[g], go.at[g], gor.at[g]).wait()
+        for j in range(2):
+
+            @pl.when(side_ok[j])
+            def _():
+                pltpu.make_async_copy(gx.at[j, g], gx.at[j, g], gxr.at[j, g]).wait()
 
     def e_halo(k, kind):
-        if kind == 0:
-            src, dst, to = eb.at[k, 0], hhi.at[k], dev(zd % 4, col * 4 + (zd // 4) * 2 + core)
-        elif kind == 1:
-            src, dst, to = eb.at[k, 1], hlo.at[k], dev(zu % 4, col * 4 + (zu // 4) * 2 + core)
-        elif kind == 2:
-            src, dst, to = eb.at[k, :, 0], hn.at[k], dev(t, prev_sp)
-        else:
-            src, dst, to = eb.at[k, :, 1], hp.at[k], dev(t, next_sp)
+        src, dst = (
+            (eb.at[k, 0], hhi.at[k]),
+            (eb.at[k, 1], hlo.at[k]),
+            (eb.at[k, :, 0], hn.at[k]),
+            (eb.at[k, :, 1], hp.at[k]),
+        )[kind]
         return pltpu.make_async_remote_copy(
             src_ref=src,
             dst_ref=dst,
             send_sem=hs.at[k, kind],
             recv_sem=hr.at[k, kind],
-            device_id=to,
+            device_id=beside[kind],
             device_id_type=MESH,
         )
 
@@ -656,6 +739,7 @@
             dev(k, sp),
         )
 
+    arrived(3)
     for b in range(2):
         for j in range(2):
             eb[0, b, j] = go[3, j, b] + gx[j, 3, b]
@@ -678,6 +762,7 @@
 
     send_level(0)
     for k in range(3):
+        arrived(k)
         e_halo(k, 0).wait_recv()
         e_halo(k, 1).wait_recv()
 
@@ -725,8 +810,15 @@
         send_level(k + 1)
 
     pltpu.make_async_copy(eout, eout, eor.at[0]).wait()
-    result = pltpu.make_async_copy(eout, out, ld_sem.at[0])
-    result.start()
+
+    @pl.loop(0, RC, unroll=4)
+    def _(r):
+        here = eout[r]
+        wide[2 * r] = here
+        wide[2 * r + 1] = here
+
+    for sl in range(8):
+        pltpu.make_async_copy(wide.at[:, sl, :], out.at[pl.ds(R * sl, R), :], ld_sem.at[0]).start()
 
     inner_c().wait_send()
     for k in range(STEPS - 2, STEPS):
@@ -751,12 +843,17 @@
                     relay(ch, i).wait_send()
 
     for h in range(2):
-        for m in range(4):
-            cross_sent(*cc_own(h, m))
-
-        @pl.when(cross_ok)
-        def _():
-            cross_sent(*cc_out(h))
+        cross_sent(*cc_own(h))
+    c_halo(0).wait_send()
+    c_halo(1).wait_send()
+
+    @pl.when(prev_ok)
+    def _():
+        c_halo(2).wait_send()
+
+    @pl.when(next_ok)
+    def _():
+        c_halo(3).wait_send()
 
     @pl.loop(0, 8)
     def _(e):
@@ -781,52 +878,45 @@
     for k in range(4):
         for j in range(2):
             cross_sent(*e_back(k, j))
-    result.wait()
-
-
-def final_kernel(itr, err, out, e, raw, res, esem, isem, osem):
+    pltpu.make_async_copy(out, out, ld_sem.at[0]).wait()
+
+
+def final_kernel(itr, e, out, res, osem):
     core = lax.axis_index("space") % 2
 
     def plane(p):
         return (3 - p) + core * (2 * p - 3)
 
-    def load(n, sl):
-        return pltpu.make_async_copy(
-            itr.at[0, :, pl.ds(R * sl + PART * n, PART), :], raw.at[n, :, :, sl, :], isem.at[n]
-        )
-
-    def store(n, sl):
-        return pltpu.make_async_copy(
-            res.at[n, :, :, sl, :], out.at[0, :, pl.ds(R * sl + PART * n, PART), :], osem.at[n]
-        )
-
-    fetch = pltpu.make_async_copy(err, e, esem.at[0])
-    fetch.start()
-    for n in range(R // PART):
-        for sl in range(8):
-            load(n, sl).start()
-    fetch.wait()
-    for n in range(R // PART):
-        pltpu.make_async_copy(raw.at[n], raw.at[n], isem.at[n]).wait()
-
-        @pl.loop(0, PART // 2, unroll=2)
-        def _(r):
-            rows = [[row(raw, n, plane(p), 2 * r + b) for b in range(2)] for p in range(4)]
-            a = add(add(*rows[0]), add(*rows[1]))
-            c = add(add(*rows[2]), add(*rows[3]))
-            d = each(lambda x, y: x - 0.125 * y, row(e, (PART // 2) * n + r), pack(a, c))
+    first = (subs((8, 128)) & 1) == 0
+
+    def row_pairs(v):
+        return [x + jnp.where(first, pltpu.roll(x, 7, axis=0), pltpu.roll(x, 1, axis=0)) for x in v]
+
+    def store(n):
+        return pltpu.make_async_copy(res.at[n], out.at[0, :, pl.ds(PART * n, PART), :], osem.at[n])
+
+    for n in range(Y // PART):
+
+        @pl.loop(0, PART // 8, unroll=2)
+        def _(i):
+            at = pl.ds(pl.multiple_of(PART * n + 8 * i, 8), 8)
+            here = pl.ds(pl.multiple_of(8 * i, 8), 8)
+            tile = lambda ref, *k: [ref[(*k, slice(128 * q, 128 * q + 128))] for q in range(LT)]
+            v = [tile(itr, 0, plane(p), at) for p in range(4)]
+            mean = pack(row_pairs(add(v[0], v[1])), row_pairs(add(v[2], v[3])))
+            d = each(lambda x, y: x - 0.125 * y, tile(e, at), mean)
             halves = (
                 [jnp.where(even(), x, pltpu.roll(x, 1, axis=1)) for x in d],
                 [jnp.where(even(), pltpu.roll(x, 127, axis=1), x) for x in d],
             )
             for p in range(4):
-                for b in range(2):
-                    put(res, add(rows[p][b], halves[p // 2]), n, plane(p), 2 * r + b)
-
-        for sl in range(8):
-            store(n, sl).start()
-    for n in range(R // PART):
-        pltpu.make_async_copy(res.at[n], res.at[n], osem.at[n]).wait()
+                new = add(v[p], halves[p // 2])
+                for q in range(LT):
+                    res[n, plane(p), here, 128 * q : 128 * q + 128] = new[q]
+
+        store(n).start()
+    for n in range(Y // PART):
+        store(n).wait()
 
 
 def local(initial, iterate, diffusivity):
@@ -835,7 +925,7 @@
     hbm = pl.BlockSpec(memory_space=pl.ANY)
     err = pl.pallas_call(
         main_kernel,
-        out_shape=jax.ShapeDtypeStruct((RC, 8, X), F32),
+        out_shape=jax.ShapeDtypeStruct((Y, X), F32),
         in_specs=[hbm] * 3,
         out_specs=hbm,
         scratch_shapes=[
@@ -863,6 +953,7 @@
             vm(3, 2, 8, X),
             vm(3, 2, 8, X),
             vm(RC, 8, X),
+            vm(R, 8, X),
             dma(2),
             dma(2),
             dma(4, CH),
@@ -871,13 +962,14 @@
             dma(STEPS),
             dma(2),
             dma(2),
-            dma(2, 5),
+            dma(2),
             dma(1),
-            dma(2),
+            dma(4),
+            dma(4),
             dma(8),
-            dma(1),
+            dma(4),
             dma(8),
-            dma(2),
+            dma(2, 4),
             dma(3, 4),
             dma(3, 4),
             dma(4, 2),
@@ -890,16 +982,9 @@
     return pl.pallas_call(
         final_kernel,
         out_shape=jax.ShapeDtypeStruct(iterate.shape, F32),
-        in_specs=[hbm, hbm],
+        in_specs=[pl.BlockSpec(memory_space=pltpu.VMEM)] * 2,
         out_specs=hbm,
-        scratch_shapes=[
-            vm(RC, 8, X),
-            vm(R // PART, 4, PART, 8, X),
-            vm(R // PART, 4, PART, 8, X),
-            dma(1),
-            dma(R // PART),
-            dma(R // PART),
-        ],
+        scratch_shapes=[vm(Y // PART, 4, PART, X), dma(Y // PART)],
         compiler_params=pltpu.CompilerParams(vmem_limit_bytes=16 * 2**20),
     )(iterate, err)
 

time: 84.7 us -> 82 us (0.968)
  Pallas kernels: 83.6 us -> 80.7 us
    pallas_call x1, Pallas kernels: 79.8 us -> 77.3 us  [local(): pl.pallas_call(main_kernel, out_shape=jax.ShapeDtypeStruct((Y, X), F32),...]
where the time goes in v3:
time: 82 us; the launch traced here: 81.8 us
  Pallas kernels  80.7 us (98%)
  local copies, waits for them, and re-layouts  1.04 us (1%)
    pallas_call x1, Pallas kernels, local(): pl.pallas_call(main_kernel, out_shape=jax.ShapeDtypeStruct((Y, X), F32),...  77.3 us
    pallas_call x1, Pallas kernels, local(): pl.pallas_call(final_kernel, out_shape=jax.ShapeDtypeStruct(iterate.shape...  3.49 us

profile of v3, /device:TPU:121, one launch (start us, length us, event | category | flops | bytes accessed | tf_op | source)
XLA Modules:
  0.0 81.8 jit_solution(2079449414103672780)
XLA Ops:
  0.0 0.0 copy-start
  0.0 77.3 %shard_map.37.e = f32[256,512]{1,0:T(8,128)} custom-call(f32[4,256,512]{2,1,0:T(8,128)} %ini.1, f32[1,4,256,512]{3,2,1,0:T(8,128)} %itr.3, f32[4,256,512]{2,1,0:T(8,128)} %dif.1), custom_call_target="tpu_custom_call" | custom-call | tf_op jit(solution)/shard_map/pallas_call | solution.py:926
  77.3 0.0 copy-done
  77.3 0.0 copy-start.1
  77.3 1.0 %copy-done.1 = f32[256,512]{1,0:T(8,128)S(1)} copy-done((f32[256,512]{1,0:T(8,128)S(1)}, f32[256,512]{1,0:T(8,128)}, u32[]{:S(2)}) %copy-start.1) | copy-done | bytes 524312
  78.3 3.5 %shard_map.38 = f32[1,4,256,512]{3,2,1,0:T(8,128)} custom-call(f32[1,4,256,512]{3,2,1,0:T(8,128)S(1)} %copy-done, f32[256,512]{1,0:T(8,128)S(1)} %copy-done.1), custom_call_target="tpu_custom_call" | custom-call | tf_op jit(solution)/shard_map/pallas_call | solution.py:982
Async XLA Ops:
  0.0 77.3 %copy-start = (f32[1,4,256,512]{3,2,1,0:T(8,128)S(1)}, f32[1,4,256,512]{3,2,1,0:T(8,128)}, u32[]{:S(2)}) copy-start(f32[1,4,256,512]{3,2,1,0:T(8,128)} %itr.3) | copy-start | bytes 6291460
  77.3 1.0 %copy-start.1 = (f32[256,512]{1,0:T(8,128)S(1)}, f32[256,512]{1,0:T(8,128)}, u32[]{:S(2)}) copy-start(f32[256,512]{1,0:T(8,128)} %shard_map.37.e) | copy-start | bytes 1572868

commit v4 on v3

--- a/solution.py
+++ b/solution.py
@@ -19,7 +19,7 @@
 RC = 16
 CH = 24
 LEAD, FAR = 5, 14
-PART = 64
+PART = 32
 
 
 PER = CH // 3
@@ -432,7 +432,7 @@
     def step_planes(k, src, dst, first, last, lo, hi):
         top = 3 + k
 
-        @pl.loop(lo, hi, unroll=2)
+        @pl.loop(lo, hi, unroll=4)
         def _(i):
             r = 2 * i
             below = [row(inn, k, r + j) if first == 0 else row(src, first - 1, r + j + 1) for j in range(2)]
@@ -533,7 +533,7 @@
         if lo == 0:
             inner_state(STEPS - 1).wait_recv()
 
-        @pl.loop(lo, hi)
+        @pl.loop(lo, hi, unroll=2)
         def _(rc):
             put(own, last_groups(2 * rc, ((0, 1),), lambda j: row(inn, STEPS - 1, 2 * rc + j))[0], rc)
 
@@ -897,7 +897,7 @@
 
     for n in range(Y // PART):
 
-        @pl.loop(0, PART // 8, unroll=2)
+        @pl.loop(0, PART // 8, unroll=4)
         def _(i):
             at = pl.ds(pl.multiple_of(PART * n + 8 * i, 8), 8)
             here = pl.ds(pl.multiple_of(8 * i, 8), 8)

time: 82 us -> 80.8 us (0.985)
  Pallas kernels: 80.7 us -> 79.6 us
where the time goes in v4:
time: 80.8 us; the launch traced here: 80.7 us
  Pallas kernels  79.6 us (99%)
  local copies, waits for them, and re-layouts  1.04 us (1%)
    pallas_call x1, Pallas kernels, local(): pl.pallas_call(main_kernel, out_shape=jax.ShapeDtypeStruct((Y, X), F32),...  76.7 us
    pallas_call x1, Pallas kernels, local(): pl.pallas_call(final_kernel, out_shape=jax.ShapeDtypeStruct(iterate.shape...  2.97 us

profile of v4, /device:TPU:121, one launch (start us, length us, event | category | flops | bytes accessed | tf_op | source)
XLA Modules:
  0.0 80.7 jit_solution(9591296537366603700)
XLA Ops:
  0.0 0.0 copy-start
  0.0 76.7 %shard_map.37.e = f32[256,512]{1,0:T(8,128)} custom-call(f32[4,256,512]{2,1,0:T(8,128)} %ini.1, f32[1,4,256,512]{3,2,1,0:T(8,128)} %itr.3, f32[4,256,512]{2,1,0:T(8,128)} %dif.1), custom_call_target="tpu_custom_call" | custom-call | tf_op jit(solution)/shard_map/pallas_call | solution.py:926
  76.7 0.0 copy-done
  76.7 0.0 copy-start.1
  76.7 1.0 %copy-done.1 = f32[256,512]{1,0:T(8,128)S(1)} copy-done((f32[256,512]{1,0:T(8,128)S(1)}, f32[256,512]{1,0:T(8,128)}, u32[]{:S(2)}) %copy-start.1) | copy-done | bytes 524312
  77.7 3.0 %shard_map.38 = f32[1,4,256,512]{3,2,1,0:T(8,128)} custom-call(f32[1,4,256,512]{3,2,1,0:T(8,128)S(1)} %copy-done, f32[256,512]{1,0:T(8,128)S(1)} %copy-done.1), custom_call_target="tpu_custom_call" | custom-call | tf_op jit(solution)/shard_map/pallas_call | solution.py:982
Async XLA Ops:
  0.0 76.7 %copy-start = (f32[1,4,256,512]{3,2,1,0:T(8,128)S(1)}, f32[1,4,256,512]{3,2,1,0:T(8,128)}, u32[]{:S(2)}) copy-start(f32[1,4,256,512]{3,2,1,0:T(8,128)} %itr.3) | copy-start | bytes 6291460
  76.7 1.0 %copy-start.1 = (f32[256,512]{1,0:T(8,128)S(1)}, f32[256,512]{1,0:T(8,128)}, u32[]{:S(2)}) copy-start(f32[256,512]{1,0:T(8,128)} %shard_map.37.e) | copy-start | bytes 1572868
